TPU v7x, 512 devices: a whole 4x8x8 slice. The times are simulated.
512 devices in a mesh: gx: 16 (over y, core), gy: 32 (over z, x).
Axes of the slice: x: 4, y: 8, z: 8, core: 2. Of those that a mesh axis runs over, the one named last changes fastest.
Arguments:
- inputs: bfloat16 [256, 4, 2304], P('gy', None, 'gx'), may hold values from -8 to 8
- cache_pool: bfloat16 [2, 64, 4096, 1024], P(None, 'gx', 'gy'), may hold values from -6 to 6
- lengths: int32 [32], P('gy'), may hold values from 1 to 32768, as said below
- block_table: int32 [32, 33], P('gy'), may hold values from -1 to 63, as said below
- parents: int32 [3, 256], P(None, 'gy'), may hold values from 0 to 7
- norm_gains: float32 [4, 2304], P(None, 'gx'), may hold values from -0.5 to 1
- w_query: bfloat16 [2304, 2048], P('gx', 'gy'), may hold values from -0.125 to 0.125
- w_key: bfloat16 [2304, 1024], P('gx', 'gy'), may hold values from -0.125 to 0.125
- w_value: bfloat16 [2304, 1024], P('gx', 'gy'), may hold values from -0.125 to 0.125
- w_out: bfloat16 [2048, 2304], P('gy', 'gx'), may hold values from -1 to 1
- w_gate: bfloat16 [2304, 9216], P('gx', 'gy'), may hold values from -0.125 to 0.125
- w_up: bfloat16 [2304, 9216], P('gx', 'gy'), may hold values from -0.125 to 0.125
- w_down: bfloat16 [9216, 2304], P('gy', 'gx'), may hold values from -1 to 1
Outputs:
- outputs: bfloat16 [256, 4, 2304], P('gy', None, 'gx')
Inputs may be any that keep to these rules, and one draw needn't show every extreme that they name: `lengths`: a group's beams share its prompt length. block_table[g, j] is the slot, numbered over the index of gy that holds group g as gx index times 4 plus the device's slot, of page first(g) + j of the group, for j up to (lengths[g] - 1) // 128 - first(g), and -1 beyond; no slot is named twice; a device holds at most 4 pages, and some device holds 4. Beam b at step s + 1 continues beam parents[s, b] of its own group, numbered within the group.
All inputs are finite; a program needn't handle non-finite values.
Results may differ from a plain program's by a relative error of at most 0.015.
Values may be sent and summed in bfloat16 or wider, within the bound.
A program may use at most 64 MiB of HBM per device.

v0:
```python
import jax
import jax.numpy as jnp
from jax import lax
from jax.sharding import PartitionSpec as P

D = 2304
HEADS = 8
KV_HEADS = 4
HEAD_DIM = 256
WINDOW = 4096
PAGE = 128
BEAM = 8


EPSILON = 1e-06
SOFT_CAP = 50.0
ROPE_BASE = 10000.0


def rotate(values, positions):
    half_width = values.shape[-1] // 2
    inverse_freq = ROPE_BASE ** (
        -jnp.arange(half_width, dtype=jnp.float32) * 2.0 / values.shape[-1]
    )
    angles = positions[..., None].astype(jnp.float32) * inverse_freq
    cosine = jnp.cos(angles)[..., None, :]
    sine_part = jnp.sin(angles)[..., None, :]
    first_half = values[..., :half_width]
    second_half = values[..., half_width:]
    return jnp.concatenate(
        [
            first_half * cosine - second_half * sine_part,
            second_half * cosine + first_half * sine_part,
        ],
        axis=-1,
    )


def ancestry(parents, beam_count, group_size, steps_count):
    beam_ids = jnp.arange(beam_count, dtype=jnp.int32)
    group_base = beam_ids // group_size * group_size
    table_rows = []
    for moment in range(steps_count):
        current = beam_ids
        chain_list = [beam_ids] * steps_count
        for earlier in range(moment, 0, -1):
            current = group_base + jnp.take(parents[earlier - 1], current)
            chain_list[earlier - 1] = current
        table_rows.append(jnp.stack(chain_list))
    return jnp.stack(table_rows)


def tail_terms(grouped, key_steps, value_steps, ancestors):
    steps_count = grouped.shape[1]
    step_ids = jnp.arange(steps_count, dtype=jnp.int32)
    tail_keys = key_steps[ancestors, step_ids[None, :, None]]
    tail_values = value_steps[ancestors, step_ids[None, :, None]]
    scores = jnp.einsum(
        "bskgd,sjbkd->bskgj", grouped, tail_keys, preferred_element_type=jnp.float32
    )
    allowed = step_ids[None, :] <= step_ids[:, None]
    weights = jnp.where(
        allowed[None, :, None, None, :], jnp.exp(SOFT_CAP * jnp.tanh(scores / SOFT_CAP)), 0.0
    )
    numerator = jnp.einsum(
        "bskgj,sjbkd->bskgd",
        weights.astype(jnp.bfloat16),
        tail_values,
        preferred_element_type=jnp.float32,
    )
    return (numerator, jnp.sum(weights, axis=-1))


def body(
    inputs,
    cache_pool,
    lengths,
    block_table,
    parents,
    norm_gains,
    w_query,
    w_key,
    w_value,
    w_out,
    w_gate,
    w_up,
    w_down,
):
    col_beams, steps_count, width_part = inputs.shape
    group_count = lengths.shape[0]
    slot_count = cache_pool.shape[1]
    rep_heads = HEADS // KV_HEADS
    x_wide = inputs.astype(jnp.float32)
    gain_rows = 1.0 + norm_gains
    square_sum = lax.psum(jnp.sum(x_wide * x_wide, axis=-1), "gx")
    normed_share = (x_wide * lax.rsqrt(square_sum / D + EPSILON)[..., None] * gain_rows[0]).astype(
        jnp.bfloat16
    )
    normed = lax.all_gather(normed_share, "gy", axis=0, tiled=True)
    all_beams = normed.shape[0]
    flat_rows = normed.reshape(-1, width_part)

    def project(weight):
        return jnp.dot(flat_rows, weight, preferred_element_type=jnp.float32).reshape(
            all_beams, steps_count, weight.shape[1]
        )

    query_sum, key_sum, value_sum = lax.psum(
        (project(w_query), project(w_key), project(w_value)), "gx"
    )
    query_raw, key_raw, value_raw = (
        lax.all_to_all(query_sum, "gy", split_axis=0, concat_axis=2, tiled=True),
        lax.all_to_all(key_sum, "gy", split_axis=0, concat_axis=2, tiled=True),
        lax.all_to_all(value_sum, "gy", split_axis=0, concat_axis=2, tiled=True),
    )
    beam_lengths = jnp.repeat(lengths, BEAM)
    step_ids = jnp.arange(steps_count, dtype=jnp.int32)
    positions = beam_lengths[:, None] + step_ids[None, :]
    queries = (
        rotate(query_raw.reshape(col_beams, steps_count, HEADS, HEAD_DIM), positions)
        * HEAD_DIM ** (-0.5)
    ).astype(jnp.bfloat16)
    key_steps = rotate(
        key_raw.reshape(col_beams, steps_count, KV_HEADS, HEAD_DIM), positions
    ).astype(jnp.bfloat16)
    value_steps = value_raw.reshape(col_beams, steps_count, KV_HEADS, HEAD_DIM).astype(jnp.bfloat16)
    grouped = queries.reshape(col_beams, steps_count, KV_HEADS, rep_heads, HEAD_DIM)
    slot_ids = lax.axis_index("gx") * slot_count + jnp.arange(slot_count, dtype=jnp.int32)
    matches = block_table[:, :, None] == slot_ids[None, None, :]
    owner_mask = jnp.any(matches, axis=1)
    slot_used = jnp.any(owner_mask, axis=0)
    page_number = jnp.sum(
        jnp.where(matches, jnp.arange(block_table.shape[1], dtype=jnp.int32)[None, :, None], 0),
        axis=(0, 1),
    )
    first_page = jnp.maximum(lengths - WINDOW + 1, 0) // PAGE
    slot_first = jnp.sum(jnp.where(owner_mask, first_page[:, None], 0), axis=0)
    slot_length = jnp.sum(jnp.where(owner_mask, lengths[:, None], 0), axis=0)
    key_positions = (slot_first + page_number)[:, None] * PAGE + jnp.arange(PAGE, dtype=jnp.int32)[
        None, :
    ]
    group_queries = grouped.reshape(group_count, BEAM, steps_count, KV_HEADS, rep_heads, HEAD_DIM)
    slot_queries = jnp.einsum(
        "an,abskgd->nbskgd",
        owner_mask.astype(jnp.bfloat16),
        group_queries,
        preferred_element_type=jnp.float32,
    ).astype(jnp.bfloat16)
    page_keys = cache_pool[0].reshape(slot_count, PAGE, KV_HEADS, HEAD_DIM)
    page_values = cache_pool[1].reshape(slot_count, PAGE, KV_HEADS, HEAD_DIM)
    scores = jnp.einsum(
        "nbskgd,ntkd->nbskgt", slot_queries, page_keys, preferred_element_type=jnp.float32
    )
    lower_bound = slot_length[:, None] + step_ids[None, :] - WINDOW + 1
    visible = (
        slot_used[:, None, None]
        & (key_positions[:, None, :] < slot_length[:, None, None])
        & (key_positions[:, None, :] >= lower_bound[:, :, None])
    )
    weights = jnp.where(
        visible[:, None, :, None, None, :], jnp.exp(SOFT_CAP * jnp.tanh(scores / SOFT_CAP)), 0.0
    )
    page_den = jnp.sum(weights, axis=-1)
    page_num = jnp.einsum(
        "nbskgt,ntkd->nbskgd",
        weights.astype(jnp.bfloat16),
        page_values,
        preferred_element_type=jnp.float32,
    )
    owner_wide = owner_mask.astype(jnp.float32)
    group_num = jnp.sum(owner_wide[:, :, None, None, None, None, None] * page_num[None], axis=1)
    group_den = jnp.sum(owner_wide[:, :, None, None, None, None] * page_den[None], axis=1)
    total_num, total_den = lax.psum((group_num, group_den), "gx")
    ancestors = ancestry(parents, col_beams, BEAM, steps_count)
    tail_num, tail_den = tail_terms(grouped, key_steps, value_steps, ancestors)
    numerator = total_num.reshape(col_beams, steps_count, KV_HEADS, rep_heads, HEAD_DIM) + tail_num
    denominator = total_den.reshape(col_beams, steps_count, KV_HEADS, rep_heads) + tail_den
    attended = (
        (numerator / denominator[..., None])
        .astype(jnp.bfloat16)
        .reshape(col_beams, steps_count, HEADS * HEAD_DIM)
    )
    head_rows = lax.all_to_all(attended, "gy", split_axis=2, concat_axis=0, tiled=True)
    head_width = head_rows.shape[2]
    attn_part = jnp.dot(
        head_rows.reshape(-1, head_width), w_out, preferred_element_type=jnp.float32
    ).reshape(all_beams, steps_count, width_part)
    attn_full = lax.psum(attn_part, "gy")
    residual = lax.all_gather(inputs, "gy", axis=0, tiled=True).astype(jnp.float32)
    attn_square = lax.psum(jnp.sum(attn_full * attn_full, axis=-1), "gx")
    mixed_full = (
        residual + attn_full * lax.rsqrt(attn_square / D + EPSILON)[..., None] * gain_rows[1]
    )
    mixed_square = lax.psum(jnp.sum(mixed_full * mixed_full, axis=-1), "gx")
    ff_input = (
        mixed_full * lax.rsqrt(mixed_square / D + EPSILON)[..., None] * gain_rows[2]
    ).astype(jnp.bfloat16)
    mixed_rows = lax.dynamic_slice_in_dim(
        mixed_full, lax.axis_index("gy") * col_beams, col_beams, 0
    )
    gate_width = w_gate.shape[1]
    matrix_rows = ff_input.reshape(-1, width_part)
    gate_and_up = jnp.concatenate(
        [
            jnp.dot(matrix_rows, w_gate, preferred_element_type=jnp.float32),
            jnp.dot(matrix_rows, w_up, preferred_element_type=jnp.float32),
        ],
        axis=1,
    )
    activate_gate_and_up = lax.psum_scatter(
        gate_and_up.reshape(ff_input.shape[0], steps_count, 2 * gate_width),
        "gx",
        scatter_dimension=0,
        tiled=True,
    )
    hidden_share = (
        jax.nn.gelu(activate_gate_and_up[..., :gate_width], approximate=True)
        * activate_gate_and_up[..., gate_width:]
    ).astype(jnp.bfloat16)
    hidden_rows = lax.all_gather(hidden_share, "gx", axis=0, tiled=True)
    down_part = jnp.dot(
        hidden_rows.reshape(-1, gate_width), w_down, preferred_element_type=jnp.float32
    ).reshape(hidden_rows.shape[0], steps_count, width_part)
    down_own = lax.psum_scatter(down_part, "gy", scatter_dimension=0, tiled=True)
    out_square = lax.psum(jnp.sum(down_own * down_own, axis=-1), "gx")
    return (
        mixed_rows + down_own * lax.rsqrt(out_square / D + EPSILON)[..., None] * gain_rows[3]
    ).astype(jnp.bfloat16)


def solution(mesh):
    return jax.shard_map(
        body,
        mesh=mesh,
        in_specs=(
            P("gy", None, "gx"),
            P(None, "gx", "gy", None),
            P("gy"),
            P("gy", None),
            P(None, "gy"),
            P(None, "gx"),
            P("gx", "gy"),
            P("gx", "gy"),
            P("gx", "gy"),
            P("gy", "gx"),
            P("gx", "gy"),
            P("gx", "gy"),
            P("gy", "gx"),
        ),
        out_specs=P("gy", None, "gx"),
        check_vma=False,
    )
```

profile of v0, /device:TPU:1, one launch (start us, length us, event | category | flops | bytes accessed | tf_op | source)
XLA Modules:
  0.0 937.2 jit_solution(2836527621570253802)
XLA Ops:
  8.1 29.8 %psum.70 = f32[8,4]{0,1:T(4,128)S(1)} all-reduce(f32[8,4]{0,1:T(4,128)S(1)} %fusion.33), channel_id=1, replica_groups=mesh['gx'=16,'gy'=32] {'gx'}, use_global_device_ids=true, to_apply=%region_3.0 | all-reduce | flops 32 | bytes 256 | tf_op jit(solution)/shard_map/psum | solution.py:95
  38.6 36.1 %all_gather.10 = bf16[256,4,144]{2,0,1:T(8,128)(2,1)S(1)} all-gather(bf16[8,4,144]{2,0,1:T(8,128)(2,1)S(1)} %fusion.35), channel_id=1, replica_groups=mesh['gx'=16,'gy'=32] {'gy'}, dimensions={0}, use_global_device_ids=true | all-gather | bytes 304128 | tf_op jit(solution)/shard_map/all_gather | solution.py:99
  84.6 111.0 %all-reduce.9.cloned.1.call-done = f32[256,4,64]{0,2,1:T(8,128)} async-done(((f32[256,4,64]{0,2,1:T(8,128)}), f32[256,4,64]{0,2,1:T(8,128)}) %all-reduce.9.cloned.1.call-update) | async-done | bytes 262160 | tf_op jit(solution)/shard_map/psum | solution.py:108
  198.0 9.9 %all-to-all-start = ((f32[32,1,2048]{2,1,0:T(1,128)}), f32[32,1,2048]{2,1,0:T(1,128)S(1)}, u32[]{:S(2)}, u32[]{:S(2)}) async-start(f32[32,1,2048]{2,1,0:T(1,128)} %reshape.614), calls=%async_computation | async-start | bytes 524288 | tf_op jit(solution)/shard_map/all_to_all | solution.py:112
  211.6 7.5 all-to-all-done
  225.1 47.4 %all-reduce.16 = (bf16[256,4,32]{0,2,1:T(8,128)(2,1)S(1)}, f32[8,4,4,2]{0,2,3,1:T(4,128)S(1)}) all-reduce(f32[256,4,32]{0,2,1:T(8,128)S(1)} %fusion.42, f32[8,4,4,2]{0,2,3,1:T(4,128)S(1)} %copy.223), channel_id=1, replica_groups=mesh['gx'=16,'gy'=32] {'gx'}, use_global_device_ids=true, to_apply=%region_8.10 | all-reduce | flops 33024 | bytes 198656 | tf_op jit(solution)/shard_map/psum | solution.py:108
  273.5 3.8 all-to-all-start.2
  278.1 120.2 %all-reduce.15.cloned.1.call-done = (f32[8,4,4,2,256]{4,3,2,1,0:T(2,128)}, f32[256,4,32]{0,2,1:T(8,128)}) async-done(((f32[8,4,4,2,256]{4,3,2,1,0:T(2,128)}, f32[256,4,32]{0,2,1:T(8,128)}), (f32[8,4,4,2,256]{4,3,2,1,0:T(2,128)}, f32[256,4,32]{0,2,1:T(8,128)})) %all-reduce.15.cloned.1.call-update) | async-done | bytes 393232 | tf_op jit(solution)/shard_map/psum | solution.py:173
  400.4 9.9 %all-to-all-start.1 = ((f32[32,1,1024]{2,1,0:T(1,128)}), f32[32,1,1024]{2,1,0:T(1,128)S(1)}, u32[]{:S(2)}, u32[]{:S(2)}) async-start(f32[32,1,1024]{2,1,0:T(1,128)} %reshape.618), calls=%async_computation.1 | async-start | bytes 262144 | tf_op jit(solution)/shard_map/all_to_all | solution.py:113
  412.2 7.5 all-to-all-done.1
  425.0 2.3 reshape.620
  427.3 12.7 %all_to_all.54 = bf16[32,2,1024]{2,1,0:T(2,128)(2,1)S(1)} all-to-all(bf16[32,2,1024]{2,1,0:T(2,128)(2,1)S(1)} %reshape.620), channel_id=1, replica_groups=mesh['gx'=16,'gy'=32] {'gy'}, dimensions={0} | all-to-all | bytes 262144 | tf_op jit(solution)/shard_map/all_to_all | solution.py:183
  440.0 2.4 reshape.621
  442.5 2.1 copy.252
  446.0 37.5 %all_gather.9 = bf16[256,4,144]{2,1,0:T(4,128)(2,1)S(1)} all-gather(bf16[8,4,144]{2,1,0:T(4,128)(2,1)S(1)} %copy-done.2), channel_id=1, replica_groups=mesh['gx'=16,'gy'=32] {'gy'}, dimensions={0}, use_global_device_ids=true | all-gather | bytes 304128 | tf_op jit(solution)/shard_map/all_gather | solution.py:189
  483.5 115.9 %all-reduce.11.cloned.1.call-done = f32[256,4,144]{2,0,1:T(8,128)} async-done(((f32[256,4,144]{2,0,1:T(8,128)}), f32[256,4,144]{2,0,1:T(8,128)}) %all-reduce.11.cloned.1.call-update) | async-done | bytes 589840 | tf_op jit(solution)/shard_map/psum | solution.py:188
  600.8 28.1 %psum.77 = f32[256,4]{0,1:T(4,128)S(1)} all-reduce(f32[256,4]{0,1:T(4,128)S(1)} %multiply_reduce_fusion.1), channel_id=1, replica_groups=mesh['gx'=16,'gy'=32] {'gx'}, use_global_device_ids=true, to_apply=%region_15.17 | all-reduce | flops 1024 | bytes 8192 | tf_op jit(solution)/shard_map/psum | solution.py:190
  630.6 23.6 %psum.78 = f32[256,4]{0,1:T(4,128)S(1)} all-reduce(f32[256,4]{0,1:T(4,128)S(1)} %get-tuple-element.12), channel_id=1, replica_groups=mesh['gx'=16,'gy'=32] {'gx'}, use_global_device_ids=true, to_apply=%region_17.19 | all-reduce | flops 1024 | bytes 8192 | tf_op jit(solution)/shard_map/psum | solution.py:194
  657.5 2.1 copy.232
  661.5 3.4 copy.233
  665.0 57.8 %reduce-scatter.2.cloned.1.call-done = f32[16,4,576]{2,0,1:T(8,128)} async-done(((f32[256,4,576]{2,0,1:T(8,128)}), f32[16,4,576]{2,0,1:T(8,128)}) %reduce-scatter.2.cloned.1.call-update) | async-done | bytes 147472 | tf_op jit(solution)/shard_map/reduce_scatter | solution.py:210
  723.9 19.0 %all_gather.11 = bf16[256,4,288]{2,0,1:T(8,128)(2,1)S(1)} all-gather(bf16[16,4,288]{2,0,1:T(8,128)(2,1)S(1)} %fusion.31), channel_id=1, replica_groups=mesh['gx'=16,'gy'=32] {'gx'}, dimensions={0}, use_global_device_ids=true | all-gather | bytes 626688 | tf_op jit(solution)/shard_map/all_gather | solution.py:220
  747.0 153.2 %all-reduce.13.cloned.1.call-done = f32[256,4,144]{2,1,0:T(4,128)} async-done(((f32[256,4,144]{2,1,0:T(4,128)}), f32[256,4,144]{2,1,0:T(4,128)}) %all-reduce.13.cloned.1.call-update) | async-done | bytes 589840
  901.1 28.1 %psum.79 = f32[8,4]{0,1:T(4,128)S(1)} all-reduce(f32[8,4]{0,1:T(4,128)S(1)} %copy.235), channel_id=1, replica_groups=mesh['gx'=16,'gy'=32] {'gx'}, use_global_device_ids=true, to_apply=%region_21.23 | all-reduce | flops 32 | bytes 256 | tf_op jit(solution)/shard_map/psum | solution.py:225
  (136 shorter events, 50.9 us)
Async XLA Ops:
  6.5 648.6 %copy-start = (bf16[144,288]{1,0:T(8,128)(2,1)S(1)}, bf16[144,288]{1,0:T(8,128)(2,1)}, u32[]{:S(2)}) copy-start(bf16[144,288]{1,0:T(8,128)(2,1)} %param.25) | copy-start | bytes 248836
  6.5 189.0 %all-reduce.9.cloned.1.call-start = ((), (), s32[]{:S(2)}) async-start(), calls=%async_computation.5 | async-start | bytes 524288 | tf_op jit(solution)/shard_map/psum | solution.py:108
  79.1 1.8 copy-start.8
  80.9 3.3 copy-start.6
  198.0 21.1 %all-to-all-start = ((f32[32,1,2048]{2,1,0:T(1,128)}), f32[32,1,2048]{2,1,0:T(1,128)S(1)}, u32[]{:S(2)}, u32[]{:S(2)}) async-start(f32[32,1,2048]{2,1,0:T(1,128)} %reshape.614), calls=%async_computation | async-start | bytes 524288 | tf_op jit(solution)/shard_map/all_to_all | solution.py:112
  208.5 2.1 copy-start.7
  273.5 126.9 %all-to-all-start.2 = ((bf16[32,2,512]{2,1,0:T(2,128)(2,1)}), bf16[32,2,512]{2,1,0:T(2,128)(2,1)S(1)}, u32[]{:S(2)}, u32[]{:S(2)}) async-start(bf16[32,2,512]{2,1,0:T(2,128)(2,1)} %reshape.616), calls=%async_computation.2 | async-start | bytes 131072 | tf_op jit(solution)/shard_map/all_to_all | solution.py:114
  277.3 121.0 %all-reduce.15.cloned.1.call-start = ((), (), s32[]{:S(2)}) async-start(), calls=%async_computation.9 | async-start | bytes 786432 | tf_op jit(solution)/shard_map/psum | solution.py:173
  400.4 19.3 %all-to-all-start.1 = ((f32[32,1,1024]{2,1,0:T(1,128)}), f32[32,1,1024]{2,1,0:T(1,128)S(1)}, u32[]{:S(2)}, u32[]{:S(2)}) async-start(f32[32,1,1024]{2,1,0:T(1,128)} %reshape.618), calls=%async_computation.1 | async-start | bytes 262144 | tf_op jit(solution)/shard_map/all_to_all | solution.py:113
  410.3 189.1 %all-reduce.11.cloned.1.call-start = ((), (), s32[]{:S(2)}) async-start(), calls=%async_computation.6 | async-start | bytes 2097152 | tf_op jit(solution)/shard_map/psum | solution.py:188
  421.3 2.0 copy-start.9
  440.0 4.6 copy-start.5
  442.5 3.5 copy-start.2
  445.9 276.9 %reduce-scatter.2.cloned.1.call-start = ((), (), s32[]{:S(2)}) async-start(), calls=%async_computation.7 | async-start | bytes 2785280 | tf_op jit(solution)/shard_map/reduce_scatter | solution.py:210
  630.6 23.8 %copy-start.1 = (f32[256,4,144]{2,0,1:T(8,128)}, f32[256,4,144]{2,0,1:T(8,128)S(1)}, u32[]{:S(2)}) copy-start(f32[256,4,144]{2,0,1:T(8,128)S(1)} %get-tuple-element.13) | copy-start | bytes 1769476
  654.4 1.1 copy-start.3
  664.9 77.9 %copy-start.4 = (bf16[288,144]{0,1:T(8,128)(2,1)S(1)}, bf16[288,144]{0,1:T(8,128)(2,1)}, u32[]{:S(2)}) copy-start(bf16[288,144]{0,1:T(8,128)(2,1)} %param.27) | copy-start | bytes 248836
  664.9 235.2 %all-reduce.13.cloned.1.call-start = ((), (), s32[]{:S(2)}) async-start(), calls=%async_computation.8 | async-start | bytes 2097152
Sparse Core Ops, SparseCore 0:
  76.6 118.8 all-reduce.8
  280.7 117.4 all-reduce.14
  446.0 153.2 all-reduce.10
  665.1 57.6 reduce-scatter.1
  745.1 154.9 all-reduce.12
where the time goes:
time: 938 us; the launch traced here: 937 us
  waiting for transfers between devices  574 us (61%)
  blocking collectives  262 us (28%)
  local copies, waits for them, and re-layouts  38.9 us (4%)
  starting transfers between devices  24 us (3%)
  between operations  15 us (2%)
  other arithmetic  14.8 us (2%)
    unnamed x6, waiting for transfers between devices  154 us
    psum x1, waiting for transfers between devices, body(): total_num, total_den = lax.psum((group_num, group_den), 'gx')  120 us
    psum x1, waiting for transfers between devices, body(): attn_full = lax.psum(attn_part, 'gy')  116 us
    psum x1, waiting for transfers between devices, body(): lax.psum((project(w_query), project(w_key), project(w_value)), 'gx')  111 us
    reduce_scatter x1, waiting for transfers between devices, body(): lax.psum_scatter(gate_and_up.reshape(ff_input.shape[0], steps_count, 2 *...  57.8 us
    psum x1, blocking collectives, body(): lax.psum((project(w_query), project(w_key), project(w_value)), 'gx')  47.4 us
    all_gather x1, blocking collectives, body(): lax.all_gather(inputs, 'gy', axis=0, tiled=True).astype(jnp.float32)  37.5 us
    all_gather x1, blocking collectives, body(): normed = lax.all_gather(normed_share, 'gy', axis=0, tiled=True)  36.1 us
  transfers between devices with their start and end apart: 8, of which 7 were waited for; matrix products, arithmetic and copies ran while one was open for 2% of the time, Pallas kernels for 0%

commit v1 on v0

v1 whole, which is shorter than its diff:
```python
import functools
import math

import jax
import jax.numpy as jnp
from jax import lax
from jax.experimental import pallas as pl
from jax.experimental.pallas import tpu as pltpu
from jax.sharding import PartitionSpec as P

MESH = pl.DeviceIdType.MESH
F32 = jnp.float32
BF16 = jnp.bfloat16

HEAD_DIM = 256
WINDOW = 4096
PAGE = 128
BEAM = 8
STEPS = 4
ROWS = BEAM * STEPS
EPSILON = 1e-06
SOFT_CAP = 50.0
ROPE_BASE = 10000.0
MAIN = 128
REST = 16

QKV_ROWS = 144
A_ROWS = 160
OUT_AT = 0
OUT_REST_AT = 64
GATE_AT = 80
DOWN_AT = 800
DOWN_REST_AT = 1088
F_ROWS = 1136
CUT = 576


def capped(scores):
    return jnp.exp(SOFT_CAP * jnp.tanh(scores * (1.0 / SOFT_CAP)))


def gelu(v):
    return 0.5 * v * (1.0 + jnp.tanh(math.sqrt(2.0 / math.pi) * (v + 0.044715 * (v * v * v))))


def dot(a, b):
    return jnp.dot(a, b, preferred_element_type=F32)


def dot_nt(a, b):
    return lax.dot_general(a, b, (((1,), (1,)), ((), ())), preferred_element_type=F32)


def layer_kernel(
    nx, ny, width,
    x_ref, wa_ref, wf_ref, cache_ref, trig_ref, table_ref, length_ref, parents_ref,
    out_ref,
    wa_all, wf_all, gain_main, gain_rest, x_in, x_own, row_out, row_all, ff_all, norm_in,
    qkv_out, qkv_in, cache, num_out, num_in, part_out, part_in, down_in, last_out, last_in,
    mixed, sums,
    cache_sem, own_sem, wa_send, wa_recv, wa_core_send, ring_send, ring_recv, wa_core_recv, wf_core_send, wf_core_recv,
    x_send, x_recv, row_send, row_recv, qkv_send, qkv_recv, num_send, num_recv,
    part_send, part_recv, ff_send, ff_recv, down_send, down_recv, last_send, last_recv,
):
    ys = nx // 2
    zs = ny // 4
    heads = ny // 4
    kv_heads = ny // 8
    tiles = nx + nx // 8 if nx >= 8 else nx + 1
    rest_tiles = tiles - nx
    blocks = 8
    i = lax.axis_index("gx")
    j = lax.axis_index("gy")
    y, c = i // 2, i % 2
    sibling = i + 1 - 2 * c
    piece = c * ys + y
    zj, xj = j // 4, j % 4
    chunk = 2 * ((zj + 2 * xj) % ys) + xj % 2
    half = xj // 2

    def group_of(part):
        x_r = 2 * part + c
        return ((y + 8 * ys - 2 * x_r) % ys) * 4 + x_r

    def owner_of(core, block):
        return 4 * block + 2 * core + block % 2 if zs == 8 else block

    if zs == 8:
        is_owner = (xj // 2 == c) & (xj % 2 == zj % 2)
        my_block = zj
    else:
        is_owner = j >= 0
        my_block = j

    def remote(src, dst, send_sem, recv_sem, tx, ty):
        return pltpu.make_async_remote_copy(
            src_ref=src, dst_ref=dst, send_sem=send_sem, recv_sem=recv_sem,
            device_id=(tx, ty), device_id_type=MESH,
        )

    def put(src, dst, send_sem, recv_sem, tx, ty):
        own = (tx == i) & (ty == j)

        @pl.when(jnp.logical_not(own))
        def _():
            remote(src, dst, send_sem, recv_sem, tx, ty).start()

        @pl.when(own)
        def _():
            pltpu.make_async_copy(src, dst, recv_sem).start()

    def take(ref, sem):
        pltpu.make_async_copy(ref, ref, sem).wait()

    def take_sent(ref, count, sem, own):
        @pl.when(own)
        def _():
            take(ref.at[pl.ds(0, count - 1)], sem)

        @pl.when(jnp.logical_not(own))
        def _():
            take(ref.at[pl.ds(0, count)], sem)

    cache_copy = pltpu.make_async_copy(cache_ref, cache, cache_sem)
    cache_copy.start()
    core_of_chunk = chunk % 2
    for q in range(4):
        put(x_ref.at[q], x_in.at[piece], x_send, x_recv, chunk, owner_of(core_of_chunk, half * 4 + q))
    for step in range(1, ys):
        remote(wa_ref, wa_all.at[c, y], wa_send, wa_recv, 2 * ((y + step) % ys) + c, j).start()
    pltpu.make_async_copy(wa_ref, wa_all.at[c, y], wa_recv).start()

    right = 2 * ((y + 1) % ys) + c
    left = 2 * ((y + ys - 1) % ys) + c
    last_step = ys // 2

    def ring_refs(step):
        from_left = (y + ys - (step - 1)) % ys
        from_right = (y + (step - 1)) % ys
        return from_left, from_right

    def ring_start(step):
        a, b = ring_refs(step)
        src_a = wf_ref if step == 1 else wf_all.at[c, a]
        src_b = wf_ref if step == 1 else wf_all.at[c, b]
        dst_a, dst_b = wf_all.at[c, a], wf_all.at[c, b]
        if step == last_step:
            src_a, dst_a = src_a.at[pl.ds(0, CUT)], dst_a.at[pl.ds(0, CUT)]
            src_b, dst_b = src_b.at[pl.ds(CUT, F_ROWS - CUT)], dst_b.at[pl.ds(CUT, F_ROWS - CUT)]
        remote(src_a, dst_a, ring_send.at[2 * step - 2], ring_recv.at[2 * step - 2], right, j).start()
        remote(src_b, dst_b, ring_send.at[2 * step - 1], ring_recv.at[2 * step - 1], left, j).start()

    def to_sibling(k):
        remote(wf_all.at[c, k], wf_all.at[c, k], wf_core_send, wf_core_recv, sibling, j).start()

    def ring_take(step):
        a = (y + ys - step) % ys
        b = (y + step) % ys
        ref_a, ref_b = wf_all.at[c, a], wf_all.at[c, b]
        if step == last_step:
            take(ref_a.at[pl.ds(0, CUT)], ring_recv.at[2 * step - 2])
            take(ref_b.at[pl.ds(CUT, F_ROWS - CUT)], ring_recv.at[2 * step - 1])
            to_sibling(a)
        else:
            take(ref_a, ring_recv.at[2 * step - 2])
            take(ref_b, ring_recv.at[2 * step - 1])
            ring_start(step + 1)
            to_sibling(a)
            to_sibling(b)

    ring_start(1)
    remote(wf_ref, wf_all.at[c, y], wf_core_send, wf_core_recv, sibling, j).start()
    own_copy = pltpu.make_async_copy(wf_ref, wf_all.at[c, y], own_sem)
    own_copy.start()

    def rest_sum(pieces):
        out = []
        for t in range(rest_tiles):
            total = None
            for k in range(min(8, nx)):
                v = pieces[8 * t + k]
                v = pltpu.roll(v, REST * k, 1) if k else v
                total = v if total is None else total + v
            out.append(total)
        return out

    def spread(which, dst_all, send_sem, recv_sem):
        @pl.loop(1, ny)
        def _(step):
            remote(row_out.at[which], dst_all.at[my_block], send_sem, recv_sem, i, (j + step) % ny).start()

        pltpu.make_async_copy(row_out.at[which], dst_all.at[my_block], recv_sem).start()

    @pl.when(is_owner)
    def _():
        take(x_in, x_recv)
        rests = []
        for p in range(nx):
            v = x_in[p].astype(F32)
            x_own[:, MAIN * p:MAIN * (p + 1)] = v[:, 0:MAIN]
            rests.append(v[:, MAIN:2 * MAIN])
        for t, v in enumerate(rest_sum(rests)):
            x_own[:, MAIN * (nx + t):MAIN * (nx + t + 1)] = v
        row_out[0] = x_own[...].astype(BF16)
        spread(0, row_all, row_send, row_recv)

    take(wa_all.at[c], wa_recv)
    remote(wa_all.at[c], wa_all.at[c], wa_core_send, wa_core_recv, sibling, j).start()
    take(wa_all.at[1 - c], wa_core_recv)
    rests = []
    for p in range(nx):
        v = wa_all[p // ys, p % ys, QKV_ROWS:A_ROWS, :].astype(F32)
        v = v[0:8] + v[8:16]
        gain_main[p] = v
        rests.append(v)
    for t, v in enumerate(rest_sum(rests)):
        gain_rest[t] = v

    def gain(which, t):
        if t < nx:
            return gain_main[t, which:which + 1, :]
        return gain_rest[t - nx, 4 + which:5 + which, :]

    if last_step > 1:
        ring_take(1)

    take(row_all, row_recv)

    def chunk_tile(ref, t):
        at = slice(MAIN * t, MAIN * (t + 1))
        return jnp.concatenate([ref[k, :, at].astype(F32) for k in range(blocks)], axis=0)

    total = None
    for t in range(tiles):
        v = chunk_tile(row_all, t)
        total = v * v if total is None else total + v * v
    scale = lax.rsqrt(jnp.sum(total, axis=1, keepdims=True) / width + EPSILON)
    for t in range(tiles):
        v = chunk_tile(row_all, t)
        norm_in[:, MAIN * t:MAIN * (t + 1)] = (v * scale * gain(0, t)).astype(BF16)
    main_w = wa_all[:, :, 0:MAIN, :].reshape(nx * MAIN, 128)
    rest_w = wa_all[:, :, MAIN:QKV_ROWS, :].reshape(nx * REST, 128)
    qkv = dot(norm_in[:, 0:nx * MAIN], main_w) + dot(norm_in[:, nx * MAIN:nx * MAIN + nx * REST], rest_w)
    qkv = qkv.astype(BF16)
    qkv_out[0] = qkv[0:ROWS]
    qkv_out[1] = qkv[ROWS:2 * ROWS]

    for part in range(2):
        group = group_of(part)

        @pl.loop(0, nx)
        def _(step):
            put(qkv_out.at[part], qkv_in.at[j], qkv_send, qkv_recv, (i + step) % nx, group)

    if last_step > 2:
        ring_take(2)

    row = lax.broadcasted_iota(jnp.int32, (ROWS, 1), 0)
    row_step, row_beam = row & 3, jnp.right_shift(row, 2)
    length = length_ref[...]
    first_page = jnp.right_shift(jnp.maximum(length - (WINDOW - 1), 0), 7).astype(F32)
    length_wide = length.astype(F32)
    page_iota = lax.broadcasted_iota(jnp.int32, table_ref.shape, 1).astype(F32)
    lane = lax.broadcasted_iota(jnp.int32, (ROWS, PAGE), 1)
    lane_wide = lane.astype(F32)
    lowest = row_step.astype(F32) - (WINDOW - 1)
    masks = []
    for slot in range(4):
        match = table_ref[...] == i * 4 + slot
        page = jnp.sum(jnp.where(match, page_iota, 0.0), axis=1, keepdims=True)
        used = jnp.sum(jnp.where(match, 1.0, 0.0), axis=1, keepdims=True)
        start = jnp.where(used > 0.5, (first_page + page) * PAGE - length_wide, 1.0)
        place = start + lane_wide
        mask = jnp.where((place < 0.0) & (place >= lowest), 1.0, 0.0)
        masks.append(jnp.concatenate([mask, mask], axis=0) > 0.5)
    key_lane = lax.broadcasted_iota(jnp.int32, (ROWS, ROWS), 1)
    key_step, key_beam = key_lane & 3, jnp.right_shift(key_lane, 2)
    beam_lane = lax.broadcasted_iota(jnp.int32, (ROWS, BEAM), 1)
    current = row_beam
    tail = jnp.zeros((ROWS, ROWS), F32)
    for at in range(STEPS - 1, -1, -1):
        hit = (key_step == at) & (row_step >= at) & (key_beam == current)
        tail = jnp.where(hit, 1.0, tail)
        if at:
            chosen = jnp.where(beam_lane == current, parents_ref[at - 1:at, :].astype(F32), 0.0)
            parent = jnp.sum(chosen, axis=1, keepdims=True).astype(jnp.int32)
            current = jnp.where(row_step >= at, parent, current)
    tail = jnp.where(i == 0, tail, 0.0)
    tail_mask = jnp.concatenate([tail, tail], axis=0) > 0.5

    cosine, sine = trig_ref[0], trig_ref[1]
    cache_copy.wait()
    take(qkv_in, qkv_recv)

    def quarter(source, at, parts):
        span = 128 // parts
        total = None
        for m in range(parts):
            v = qkv_in[source + m].astype(F32)
            shift = (span * m - at) % 128
            v = pltpu.roll(v, shift, 1) if shift else v
            total = v if total is None else jnp.where(lane >= span * m, v, total)
        return total

    def rotated(u, w):
        return u * cosine - w * sine, w * cosine + u * sine

    def wide(u, w):
        return jnp.concatenate([u, w], axis=1)

    for h in range(kv_heads):
        qs = []
        for g in range(2):
            base = 4 * (2 * h + g)
            u, w = rotated(quarter(base, 0, 2), quarter(base + 2, 0, 2))
            qs.append(wide(u, w) * HEAD_DIM ** -0.5)
        query = jnp.concatenate(qs, axis=0).astype(BF16)
        key = wide(*rotated(quarter(8 * h, 64, 4), quarter(8 * h + 4, 64, 4))).astype(BF16)
        value = wide(quarter(8 * h, 96, 4), quarter(8 * h + 4, 96, 4)).astype(BF16)
        weights = jnp.where(tail_mask, capped(dot_nt(query, key)), 0.0)
        den = jnp.sum(weights, axis=1, keepdims=True)
        num = dot(weights.astype(BF16), value)
        for slot in range(4):
            at = slice(HEAD_DIM * h, HEAD_DIM * (h + 1))
            weights = jnp.where(masks[slot], capped(dot_nt(query, cache[0, slot, :, at])), 0.0)
            den = den + jnp.sum(weights, axis=1, keepdims=True)
            num = num + dot(weights.astype(BF16), cache[1, slot, :, at])
        den_high = den.astype(BF16).astype(F32)
        den_low = den - den_high
        for g in range(2):
            rows = slice(ROWS * g, ROWS * (g + 1))
            both = jnp.where(lane < 96, den_high[rows], den_low[rows])
            for t in range(2):
                v = num[rows, 128 * t:128 * (t + 1)]
                base = 4 * (2 * h + g) + 2 * t
                num_out[base] = jnp.where(lane < 64, v, both).astype(BF16)
                num_out[base + 1] = jnp.where(lane < 64, pltpu.roll(v, 64, 1), both).astype(BF16)

    @pl.loop(0, ny)
    def _(step):
        to = (j + step) % ny
        put(num_out.at[to], num_in.at[half, piece], num_send, num_recv, chunk, to)

    for step in range(3, last_step):
        ring_take(step)
    own_copy.wait()

    take(num_in, num_recv)
    attended = []
    for part in range(2):
        total = None
        for p in range(nx):
            v = num_in[part, p].astype(F32)
            total = v if total is None else total + v
        attended.append(total[:, 0:64] / (total[:, 64:65] + total[:, 96:97]))
    attended = jnp.concatenate(attended, axis=0).astype(BF16)
    ring_take(last_step)
    take(wf_all.at[1 - c], wf_core_recv)

    def put_partial(which, t, v):
        for k in range(blocks):
            part_out[which, k, :, MAIN * t:MAIN * (t + 1)] = v[8 * k:8 * (k + 1)].astype(BF16)

    def put_rest(which, v):
        if v.shape[1] < 128:
            v = jnp.concatenate([v, jnp.zeros((v.shape[0], 128 - v.shape[1]), F32)], axis=1)
        for t in range(rest_tiles):
            put_partial(which, nx + t, v[:, 128 * t:128 * (t + 1)])

    for p in range(nx):
        put_partial(0, p, dot(attended, wf_all[p // ys, p % ys, OUT_AT:OUT_REST_AT, :]))
    rest_w = wf_all[:, :, OUT_REST_AT:GATE_AT, :].reshape(nx * REST, 128)
    put_rest(0, dot_nt(attended, rest_w[:, 0:64]))

    def send_partial(which, dst_all, send_sem, recv_sem):
        @pl.loop(0, blocks)
        def _(k):
            put(part_out.at[which, k], dst_all.at[j], send_sem, recv_sem, i, owner_of(c, k))

    def add_up(ref, t):
        total = None
        for s in range(ny):
            v = ref[s, :, MAIN * t:MAIN * (t + 1)].astype(F32)
            total = v if total is None else total + v
        return total

    def add_rows(ref):
        square = None
        for t in range(tiles):
            v = add_up(ref, t)
            sums[:, MAIN * t:MAIN * (t + 1)] = v
            square = v * v if square is None else square + v * v
        return lax.rsqrt(jnp.sum(square, axis=1, keepdims=True) / width + EPSILON)

    send_partial(0, part_in, part_send, part_recv)

    @pl.when(is_owner)
    def _():
        take(part_in, part_recv)
        scale = add_rows(part_in)
        square = None
        for t in range(tiles):
            at = slice(MAIN * t, MAIN * (t + 1))
            v = x_own[:, at] + sums[:, at] * scale * gain(1, t)
            mixed[:, at] = v
            square = v * v if square is None else square + v * v
        scale = lax.rsqrt(jnp.sum(square, axis=1, keepdims=True) / width + EPSILON)
        for t in range(tiles):
            at = slice(MAIN * t, MAIN * (t + 1))
            row_out[1, :, at] = (mixed[:, at] * scale * gain(2, t)).astype(BF16)

        spread(1, ff_all, ff_send, ff_recv)

    take(ff_all, ff_recv)
    for t in range(tiles):
        norm_in[:, MAIN * t:MAIN * (t + 1)] = chunk_tile(ff_all, t).astype(BF16)
    main_x = norm_in[:, 0:nx * MAIN]
    rest_x = norm_in[:, nx * MAIN:nx * MAIN + nx * REST]

    def ff_part(n):
        at = GATE_AT + 144 * n
        main_w = wf_all[:, :, at:at + MAIN, :].reshape(nx * MAIN, 128)
        rest_w = wf_all[:, :, at + MAIN:at + 144, :].reshape(nx * REST, 128)
        return dot(main_x, main_w) + dot(rest_x, rest_w)

    hidden = [(gelu(ff_part(n)) * ff_part(n + 2)).astype(BF16) for n in range(2)]
    both = ff_part(4)
    narrow = gelu(both) * pltpu.roll(both, 96, 1)
    lane_chunk = lax.broadcasted_iota(jnp.int32, narrow.shape, 1)
    hidden.append(jnp.where(lane_chunk < 32, narrow, 0.0).astype(BF16))
    first_hidden = jnp.concatenate(hidden[0:2], axis=1)
    for p in range(nx):
        w = wf_all.at[p // ys, p % ys]
        v = dot(first_hidden, w[DOWN_AT:DOWN_AT + 256, :])
        v = v + dot(hidden[2][:, 0:32], w[DOWN_AT + 256:DOWN_REST_AT, :])
        put_partial(1, p, v)
    v = None
    for n in range(3):
        at = DOWN_REST_AT + REST * n
        rest_w = wf_all[:, :, at:at + REST, :].reshape(nx * REST, 128)
        term = dot_nt(hidden[n], rest_w)
        v = term if v is None else v + term
    put_rest(1, v)
    send_partial(1, down_in, down_send, down_recv)

    @pl.when(is_owner)
    def _():
        take(down_in, down_recv)
        scale = add_rows(down_in)

        def result(t):
            at = slice(MAIN * t, MAIN * (t + 1))
            return mixed[:, at] + sums[:, at] * scale * gain(3, t)

        for p in range(nx):
            v = result(nx + p // 8)
            shift = (128 - REST * (p % 8)) % 128
            v = pltpu.roll(v, shift, 1) if shift else v
            last_out[p] = jnp.concatenate([result(p), v], axis=1).astype(BF16)
        group = group_of(my_block // 4)

        @pl.loop(0, nx)
        def _(p):
            to = 2 * (p % ys) + p // ys
            put(last_out.at[p], last_in.at[my_block % 4], last_send, last_recv, to, group)

    take(last_in, last_recv)
    out_ref[...] = last_in[...]

    home = chunk == i
    take_sent(x_in, 4, x_send, home & is_owner & (my_block // 4 == half))
    if ys > 1:
        take(wa_all.at[c, pl.ds(0, ys - 1)], wa_send)
    take(wa_all.at[c], wa_core_send)
    for step in range(1, last_step + 1):
        for side in range(2):
            rows = pl.ds(0, F_ROWS) if step < last_step else pl.ds(CUT * side, F_ROWS - CUT if side else CUT)
            take(wf_all.at[0, 0, rows], ring_send.at[2 * step - 2 + side])
    take(wf_all.at[c], wf_core_send)
    take_sent(qkv_in, ny, qkv_send, home)
    take_sent(num_out, ny, num_send, home)
    take_sent(row_all, blocks, part_send, is_owner)
    take_sent(ff_all, blocks, down_send, is_owner)

    @pl.when(is_owner)
    def _():
        take(part_in.at[pl.ds(0, ny - 1)], row_send)
        take(down_in.at[pl.ds(0, ny - 1)], ff_send)
        take_sent(x_in, nx, last_send, home & (my_block // 4 == half))


def body(
    inputs, cache_pool, lengths, block_table, parents, norm_gains,
    w_query, w_key, w_value, w_out, w_gate, w_up, w_down, *, nx, ny,
):
    columns = inputs.shape[2]
    tiles = nx + max(nx // 8, 1)
    rest_tiles = tiles - nx
    span = tiles * MAIN
    ys = nx // 2
    last_step = ys // 2

    x = jnp.pad(inputs.reshape(ROWS // 8, 8, columns), ((0, 0), (0, 0), (0, 256 - columns)))
    gains = 1.0 + norm_gains
    gains = jnp.concatenate([gains[:, 0:MAIN], jnp.pad(gains[:, MAIN:], ((0, 0), (0, MAIN - REST)))], axis=0)
    high = lax.reduce_precision(gains, 8, 7)
    qkv_weights = jnp.concatenate([w_query, w_key, w_value], axis=1)
    wa = jnp.concatenate([qkv_weights, high.astype(BF16), (gains - high).astype(BF16)], axis=0)
    narrow = jnp.pad(jnp.concatenate([w_gate[:, 256:], w_up[:, 256:]], axis=1), ((0, 0), (0, 64)))
    out_rest = jnp.pad(w_out[:, MAIN:].T, ((0, 0), (0, 64)))
    down_rest = jnp.pad(w_down[:, MAIN:].T, ((0, 0), (0, 96)))
    wf = jnp.concatenate(
        [w_out[:, 0:MAIN], out_rest]
        + [w_gate[:, 0:128], w_gate[:, 128:256], w_up[:, 0:128], w_up[:, 128:256], narrow]
        + [w_down[:, 0:MAIN]] + [down_rest[:, 128 * n:128 * (n + 1)] for n in range(3)],
        axis=0,
    )
    frequency = ROPE_BASE ** (-jnp.arange(128, dtype=F32) * 2.0 / HEAD_DIM)
    positions = lengths[0] + jnp.arange(STEPS, dtype=jnp.int32)
    angles = positions[:, None].astype(F32) * frequency
    trig = jnp.tile(jnp.stack([jnp.cos(angles), jnp.sin(angles)]), (1, BEAM, 1))

    vmem = pl.BlockSpec(memory_space=pltpu.VMEM)
    dma = pltpu.SemaphoreType.DMA
    out = pl.pallas_call(
        functools.partial(layer_kernel, nx, ny, nx * columns),
        name="layer",
        out_shape=jax.ShapeDtypeStruct((4, 8, 256), BF16),
        in_specs=[vmem, vmem, vmem, pl.BlockSpec(memory_space=pl.ANY), vmem, vmem, vmem, vmem],
        out_specs=vmem,
        scratch_shapes=[
            pltpu.VMEM((2, ys, A_ROWS, 128), BF16),
            pltpu.VMEM((2, ys, F_ROWS, 128), BF16),
            pltpu.VMEM((nx, 8, 128), F32),
            pltpu.VMEM((rest_tiles, 8, 128), F32),
            pltpu.VMEM((nx, 8, 256), BF16),
            pltpu.VMEM((8, span), F32),
            pltpu.VMEM((2, 8, span), BF16),
            pltpu.VMEM((8, 8, span), BF16),
            pltpu.VMEM((8, 8, span), BF16),
            pltpu.VMEM((64, span), BF16),
            pltpu.VMEM((2, ROWS, 128), BF16),
            pltpu.VMEM((ny, ROWS, 128), BF16),
            pltpu.VMEM(cache_pool.shape, BF16),
            pltpu.VMEM((ny, ROWS, 128), BF16),
            pltpu.VMEM((2, nx, ROWS, 128), BF16),
            pltpu.VMEM((2, 8, 8, span), BF16),
            pltpu.VMEM((ny, 8, span), BF16),
            pltpu.VMEM((ny, 8, span), BF16),
            pltpu.VMEM((nx, 8, 256), BF16),
            pltpu.VMEM((4, 8, 256), BF16),
            pltpu.VMEM((8, span), F32),
            pltpu.VMEM((8, span), F32),
        ]
        + [dma(())] * 5
        + [dma((2 * last_step,)), dma((2 * last_step,))]
        + [dma(())] * 19,
        compiler_params=pltpu.CompilerParams(has_side_effects=True, vmem_limit_bytes=40 << 20),
    )(x, wa, wf, cache_pool, trig, block_table, lengths.reshape(1, 1), parents)
    return out[:, :, 0:columns].reshape(inputs.shape)


def solution(mesh):
    return jax.shard_map(
        functools.partial(body, nx=mesh.shape["gx"], ny=mesh.shape["gy"]),
        mesh=mesh,
        in_specs=(
            P("gy", None, "gx"),
            P(None, "gx", "gy", None),
            P("gy"),
            P("gy", None),
            P(None, "gy"),
            P(None, "gx"),
            P("gx", "gy"),
            P("gx", "gy"),
            P("gx", "gy"),
            P("gy", "gx"),
            P("gx", "gy"),
            P("gx", "gy"),
            P("gy", "gx"),
        ),
        out_specs=P("gy", None, "gx"),
        check_vma=False,
    )
```

time: 938 us -> 151 us (0.16)
  the two profiles are of different devices: /device:TPU:1 before, /device:TPU:69 now
where the time goes in v1:
time: 151 us; the launch traced here: 150 us
  Pallas kernels  133 us (88%)
  local copies, waits for them, and re-layouts  14.8 us (10%)
    pallas_call x1, Pallas kernels, body(): pl.pallas_call(functools.partial(layer_kernel, nx, ny, nx * columns), nam...  133 us
    unnamed x20, local copies, waits for them, and re-layouts  9.54 us

profile of v1, /device:TPU:69, one launch (start us, length us, event | category | flops | bytes accessed | tf_op | source)
XLA Modules:
  0.0 149.9 jit_solution(10861195318634317624)
XLA Ops:
  0.0 0.7 slice_bitcast_fusion
  0.7 0.7 constant_dynamic-update-slice_fusion.5
  1.4 0.7 slice.53
  2.2 0.8 slice_dynamic-update-slice_fusion.3
  3.0 0.8 slice_dynamic-update-slice_fusion.2
  3.8 0.8 slice_dynamic-update-slice_fusion.1
  4.6 0.8 slice_dynamic-update-slice_fusion
  5.4 0.8 slice.58
  6.1 0.8 slice.59
  6.9 0.1 fusion.3
  7.0 0.9 slice.60
  7.9 0.1 copy.20
  8.1 0.7 broadcast_add_fusion
  8.8 0.9 copy.14
  9.7 0.8 copy.15
  10.5 0.8 copy.16
  11.3 0.1 pad_maximum_fusion.wa_ref
  12.1 0.1 multiply_cosine_fusion
  12.3 0.7 reshape.114
  13.0 1.6 %copy-done = bf16[2,4,128,1024]{3,2,1,0:T(8,128)(2,1)S(1)} copy-done((bf16[2,4,128,1024]{3,2,1,0:T(8,128)(2,1)S(1)}, bf16[2,4,128,1024]{3,2,1,0:T(8,128)(2,1)}, u32[]{:S(2)}) %copy-start) | copy-done | bytes 2097176
  14.6 0.7 copy-done.1
  15.3 0.7 copy-done.2
  16.0 133.3 %layer.1 = bf16[4,8,256]{2,1,0:T(8,128)(2,1)S(1)} custom-call(bf16[4,8,256]{2,1,0:T(8,128)(2,1)S(1)} %pad.20.x_ref, bf16[160,128]{1,0:T(8,128)(2,1)S(1)} %pad_maximum_fusion.wa_ref, bf16[1136,128]{1,0:T(8,128)(2,1)S(1)} %constant_dynamic-update-slice_fusion.wf_ref, bf16[2,4,128,1024]{3,2,1,0:T(8,128)(2,1)S(1)} %copy-done, f32[2,32,128]{2,1,0:T(8,128)S(1)} %bitcast.9, ...), custom_call_target="tpu_custom_call" | custom-call | tf_op jit(solution)/shard_map/layer/pallas_call | solution.py:525
  149.3 0.6 reshape.116
  (17 shorter events, 0.2 us)
Async XLA Ops:
  13.0 1.6 %copy-start = (bf16[2,4,128,1024]{3,2,1,0:T(8,128)(2,1)S(1)}, bf16[2,4,128,1024]{3,2,1,0:T(8,128)(2,1)}, u32[]{:S(2)}) copy-start(bf16[2,4,128,1024]{3,2,1,0:T(8,128)(2,1)} %cache_ref.1) | copy-start | bytes 6291460
  14.6 0.7 copy-start.1
  15.3 0.7 copy-start.2

commit v2 on v1

--- a/solution.py
+++ b/solution.py
@@ -29,10 +29,11 @@
 OUT_AT = 0
 OUT_REST_AT = 64
 GATE_AT = 80
+NARROW_AT = 656
 DOWN_AT = 800
-DOWN_REST_AT = 1088
-F_ROWS = 1136
-CUT = 576
+F_ROWS = 1088
+CUT = 544
+DEN_ROWS = 40
 
 
 def capped(scores):
@@ -53,22 +54,26 @@
 
 def layer_kernel(
     nx, ny, width,
-    x_ref, wa_ref, wf_ref, cache_ref, trig_ref, table_ref, length_ref, parents_ref,
+    inputs_ref, cache_ref, length_ref, table_ref, parents_ref, gains_ref,
+    wq_ref, wk_ref, wv_ref, wo_ref, wg_ref, wu_ref, wd_ref, trig_ref,
     out_ref,
-    wa_all, wf_all, gain_main, gain_rest, x_in, x_own, row_out, row_all, ff_all, norm_in,
-    qkv_out, qkv_in, cache, num_out, num_in, part_out, part_in, down_in, last_out, last_in,
+    inputs_vm, cache, table_vm, parents_vm, gains_vm,
+    wq_vm, wk_vm, wv_vm, wo_vm, wg_vm, wu_vm, wd_vm,
+    wa_all, wf_all, gain_main, gain_rest, x_out, x_in, x_own, row_all, ff_all, norm_in,
+    qkv_out, qkv_in, num_out, num_in, att_out, att_in, part_out, part_in, down_in, last_out, last_in,
     mixed, sums,
-    cache_sem, own_sem, wa_send, wa_recv, wa_core_send, ring_send, ring_recv, wa_core_recv, wf_core_send, wf_core_recv,
-    x_send, x_recv, row_send, row_recv, qkv_send, qkv_recv, num_send, num_recv,
-    part_send, part_recv, ff_send, ff_recv, down_send, down_recv, last_send, last_recv,
+    load_sem, wa_send, wa_recv, wa_core_send, wa_core_recv, ring_send, ring_recv, wf_core_send, wf_core_recv,
+    x_send, x_recv, row_a_send, row_a_recv, row_b_send, row_b_recv, qkv_send, qkv_recv, num_send, num_recv,
+    att_send, att_recv, part_send, part_recv, ff_a_send, ff_a_recv, ff_b_send, ff_b_recv,
+    down_send, down_recv, last_send, last_recv,
 ):
     ys = nx // 2
     zs = ny // 4
-    heads = ny // 4
     kv_heads = ny // 8
     tiles = nx + nx // 8 if nx >= 8 else nx + 1
     rest_tiles = tiles - nx
     blocks = 8
+    row_blocks = blocks // zs
     i = lax.axis_index("gx")
     j = lax.axis_index("gy")
     y, c = i // 2, i % 2
@@ -121,14 +126,72 @@
         def _():
             take(ref.at[pl.ds(0, count)], sem)
 
-    cache_copy = pltpu.make_async_copy(cache_ref, cache, cache_sem)
-    cache_copy.start()
+    loads = [
+        pltpu.make_async_copy(src, dst, load_sem.at[k])
+        for k, (src, dst) in enumerate([
+            (inputs_ref, inputs_vm), (wq_ref, wq_vm), (wk_ref, wk_vm), (wv_ref, wv_vm), (gains_ref, gains_vm),
+            (wo_ref, wo_vm), (wg_ref, wg_vm), (wu_ref, wu_vm), (wd_ref, wd_vm),
+            (table_ref, table_vm), (parents_ref, parents_vm), (cache_ref, cache),
+        ])
+    ]
+    for load in loads:
+        load.start()
+
+    home = chunk == i
+    own_rows = home & is_owner & (my_block // 4 == half)
+    barrier = pltpu.get_barrier_semaphore()
+
+    def hello(tx, ty):
+        pl.semaphore_signal(barrier, inc=1, device_id=(tx, ty), device_id_type=MESH)
+
+    for step in range(1, ys):
+        hello(2 * ((y + step) % ys) + c, j)
+    hello(sibling, j)
+    for step in range(1, zs):
+        hello(i, 4 * ((zj + step) % zs) + xj)
+    for step in range(1, 4):
+        if zs == 8:
+            @pl.when((2 * c + zj % 2) == (xj + step) % 4)
+            def _():
+                hello(i, 4 * zj + (xj + step) % 4)
+        else:
+            hello(i, 4 * zj + (xj + step) % 4)
+
+    @pl.when(is_owner)
+    def _():
+        group = group_of(my_block // 4)
+
+        @pl.loop(0, nx)
+        def _(to):
+            @pl.when(jnp.logical_not((to == i) & (group == j)))
+            def _():
+                hello(to, group)
+
+    waits = ys + (zs - 1) + 4
+    waits = waits + jnp.where(is_owner, 3, 0) - jnp.where(own_rows, 1, 0)
+
+    loads[0].wait()
+    for q in range(4):
+        v = jnp.concatenate([inputs_vm[2 * q].astype(F32), inputs_vm[2 * q + 1].astype(F32)], axis=0)
+        v = jnp.concatenate([v, jnp.zeros((8, MAIN - REST), F32)], axis=1)
+        x_out[q] = v.astype(BF16)
+    pl.semaphore_wait(barrier, waits)
     core_of_chunk = chunk % 2
     for q in range(4):
-        put(x_ref.at[q], x_in.at[piece], x_send, x_recv, chunk, owner_of(core_of_chunk, half * 4 + q))
+        put(x_out.at[q], x_in.at[piece], x_send, x_recv, chunk, owner_of(core_of_chunk, half * 4 + q))
+    for load in loads[1:5]:
+        load.wait()
+    v = jnp.concatenate([wq_vm[...].astype(F32), wk_vm[...].astype(F32), wv_vm[...].astype(F32)], axis=0)
+    wa_all[c, y, 0:MAIN, :] = v[:, 0:MAIN].T.astype(BF16)
+    v = jnp.concatenate([v[:, MAIN:], jnp.zeros((128, MAIN - REST), F32)], axis=1).T
+    wa_all[c, y, MAIN:QKV_ROWS, :] = v[0:REST].astype(BF16)
+    v = 1.0 + gains_vm[...]
+    v = jnp.concatenate([v, jnp.zeros((4, MAIN - REST), F32)], axis=1)
+    v = jnp.concatenate([v[:, 0:MAIN], v[:, MAIN:]], axis=0)
+    high = v.astype(BF16).astype(F32)
+    wa_all[c, y, QKV_ROWS:A_ROWS, :] = jnp.concatenate([high, v - high], axis=0).astype(BF16)
     for step in range(1, ys):
-        remote(wa_ref, wa_all.at[c, y], wa_send, wa_recv, 2 * ((y + step) % ys) + c, j).start()
-    pltpu.make_async_copy(wa_ref, wa_all.at[c, y], wa_recv).start()
+        remote(wa_all.at[c, y], wa_all.at[c, y], wa_send, wa_recv, 2 * ((y + step) % ys) + c, j).start()
 
     right = 2 * ((y + 1) % ys) + c
     left = 2 * ((y + ys - 1) % ys) + c
@@ -141,14 +204,11 @@
 
     def ring_start(step):
         a, b = ring_refs(step)
-        src_a = wf_ref if step == 1 else wf_all.at[c, a]
-        src_b = wf_ref if step == 1 else wf_all.at[c, b]
-        dst_a, dst_b = wf_all.at[c, a], wf_all.at[c, b]
+        src_a, src_b = wf_all.at[c, a], wf_all.at[c, b]
         if step == last_step:
-            src_a, dst_a = src_a.at[pl.ds(0, CUT)], dst_a.at[pl.ds(0, CUT)]
-            src_b, dst_b = src_b.at[pl.ds(CUT, F_ROWS - CUT)], dst_b.at[pl.ds(CUT, F_ROWS - CUT)]
-        remote(src_a, dst_a, ring_send.at[2 * step - 2], ring_recv.at[2 * step - 2], right, j).start()
-        remote(src_b, dst_b, ring_send.at[2 * step - 1], ring_recv.at[2 * step - 1], left, j).start()
+            src_a, src_b = src_a.at[pl.ds(0, CUT)], src_b.at[pl.ds(CUT, F_ROWS - CUT)]
+        remote(src_a, src_a, ring_send.at[2 * step - 2], ring_recv.at[2 * step - 2], right, j).start()
+        remote(src_b, src_b, ring_send.at[2 * step - 1], ring_recv.at[2 * step - 1], left, j).start()
 
     def to_sibling(k):
         remote(wf_all.at[c, k], wf_all.at[c, k], wf_core_send, wf_core_recv, sibling, j).start()
@@ -168,11 +228,6 @@
             to_sibling(a)
             to_sibling(b)
 
-    ring_start(1)
-    remote(wf_ref, wf_all.at[c, y], wf_core_send, wf_core_recv, sibling, j).start()
-    own_copy = pltpu.make_async_copy(wf_ref, wf_all.at[c, y], own_sem)
-    own_copy.start()
-
     def rest_sum(pieces):
         out = []
         for t in range(rest_tiles):
@@ -184,12 +239,25 @@
             out.append(total)
         return out
 
-    def spread(which, dst_all, send_sem, recv_sem):
-        @pl.loop(1, ny)
-        def _(step):
-            remote(row_out.at[which], dst_all.at[my_block], send_sem, recv_sem, i, (j + step) % ny).start()
-
-        pltpu.make_async_copy(row_out.at[which], dst_all.at[my_block], recv_sem).start()
+    def spread(ref, send_sem, recv_sem):
+        for step in range(1, 4):
+            src = ref.at[my_block]
+            remote(src, src, send_sem, recv_sem, i, 4 * zj + (xj + step) % 4).start()
+
+    def spread_in(ref, recv_sem):
+        @pl.when(jnp.logical_not(is_owner))
+        def _():
+            take(ref.at[pl.ds(0, row_blocks)], recv_sem)
+
+        if row_blocks > 1:
+            @pl.when(is_owner)
+            def _():
+                take(ref.at[pl.ds(0, row_blocks - 1)], recv_sem)
+
+    def spread_out(ref, send_sem, recv_sem):
+        src = ref.at[pl.ds(row_blocks * zj, row_blocks)]
+        for step in range(1, zs):
+            remote(src, src, send_sem, recv_sem, i, 4 * ((zj + step) % zs) + xj).start()
 
     @pl.when(is_owner)
     def _():
@@ -201,10 +269,30 @@
             rests.append(v[:, MAIN:2 * MAIN])
         for t, v in enumerate(rest_sum(rests)):
             x_own[:, MAIN * (nx + t):MAIN * (nx + t + 1)] = v
-        row_out[0] = x_own[...].astype(BF16)
-        spread(0, row_all, row_send, row_recv)
-
-    take(wa_all.at[c], wa_recv)
+        row_all[my_block] = x_own[...].astype(BF16)
+        spread(row_all, row_a_send, row_a_recv)
+
+    for load in loads[5:9]:
+        load.wait()
+    own_f = wf_all.at[c, y]
+    own_f[OUT_AT:OUT_REST_AT, :] = wo_vm[:, 0:MAIN]
+    v = jnp.concatenate([wo_vm[:, MAIN:].astype(F32), jnp.zeros((64, MAIN - REST), F32)], axis=1)
+    v = jnp.concatenate([v, jnp.zeros((64, MAIN), F32)], axis=0).T
+    own_f[OUT_REST_AT:GATE_AT, :] = v[0:REST].astype(BF16)
+    for n in range(2):
+        at = slice(MAIN * n, MAIN * (n + 1))
+        own_f[GATE_AT + 144 * n:GATE_AT + 144 * (n + 1), :] = wg_vm[:, at]
+        own_f[GATE_AT + 144 * (n + 2):GATE_AT + 144 * (n + 3), :] = wu_vm[:, at]
+        own_f[DOWN_AT + 144 * n:DOWN_AT + 144 * (n + 1), :] = wd_vm[:, at]
+    v = [w[:, 256:288].astype(F32) for w in (wg_vm, wu_vm, wd_vm)] + [jnp.zeros((144, 32), F32)]
+    own_f[NARROW_AT:DOWN_AT, :] = jnp.concatenate(v, axis=1).astype(BF16)
+    ring_start(1)
+    to_sibling(y)
+
+    spread_in(row_all, row_a_recv)
+    spread_out(row_all, row_b_send, row_b_recv)
+
+    take(wa_all.at[c, pl.ds(0, ys - 1)], wa_recv)
     remote(wa_all.at[c], wa_all.at[c], wa_core_send, wa_core_recv, sibling, j).start()
     take(wa_all.at[1 - c], wa_core_recv)
     rests = []
@@ -221,10 +309,7 @@
             return gain_main[t, which:which + 1, :]
         return gain_rest[t - nx, 4 + which:5 + which, :]
 
-    if last_step > 1:
-        ring_take(1)
-
-    take(row_all, row_recv)
+    take(row_all.at[pl.ds(0, blocks - row_blocks)], row_b_recv)
 
     def chunk_tile(ref, t):
         at = slice(MAIN * t, MAIN * (t + 1))
@@ -252,21 +337,23 @@
         def _(step):
             put(qkv_out.at[part], qkv_in.at[j], qkv_send, qkv_recv, (i + step) % nx, group)
 
-    if last_step > 2:
-        ring_take(2)
+    if last_step > 1:
+        ring_take(1)
 
     row = lax.broadcasted_iota(jnp.int32, (ROWS, 1), 0)
     row_step, row_beam = row & 3, jnp.right_shift(row, 2)
-    length = length_ref[...]
+    for load in loads[9:12]:
+        load.wait()
+    length = jnp.full((1, 1), length_ref[0], jnp.int32)
     first_page = jnp.right_shift(jnp.maximum(length - (WINDOW - 1), 0), 7).astype(F32)
     length_wide = length.astype(F32)
-    page_iota = lax.broadcasted_iota(jnp.int32, table_ref.shape, 1).astype(F32)
+    page_iota = lax.broadcasted_iota(jnp.int32, table_vm.shape, 1).astype(F32)
     lane = lax.broadcasted_iota(jnp.int32, (ROWS, PAGE), 1)
     lane_wide = lane.astype(F32)
     lowest = row_step.astype(F32) - (WINDOW - 1)
     masks = []
     for slot in range(4):
-        match = table_ref[...] == i * 4 + slot
+        match = table_vm[...] == i * 4 + slot
         page = jnp.sum(jnp.where(match, page_iota, 0.0), axis=1, keepdims=True)
         used = jnp.sum(jnp.where(match, 1.0, 0.0), axis=1, keepdims=True)
         start = jnp.where(used > 0.5, (first_page + page) * PAGE - length_wide, 1.0)
@@ -282,14 +369,13 @@
         hit = (key_step == at) & (row_step >= at) & (key_beam == current)
         tail = jnp.where(hit, 1.0, tail)
         if at:
-            chosen = jnp.where(beam_lane == current, parents_ref[at - 1:at, :].astype(F32), 0.0)
+            chosen = jnp.where(beam_lane == current, parents_vm[at - 1:at, :].astype(F32), 0.0)
             parent = jnp.sum(chosen, axis=1, keepdims=True).astype(jnp.int32)
             current = jnp.where(row_step >= at, parent, current)
     tail = jnp.where(i == 0, tail, 0.0)
     tail_mask = jnp.concatenate([tail, tail], axis=0) > 0.5
 
     cosine, sine = trig_ref[0], trig_ref[1]
-    cache_copy.wait()
     take(qkv_in, qkv_recv)
 
     def quarter(source, at, parts):
@@ -329,30 +415,38 @@
         den_low = den - den_high
         for g in range(2):
             rows = slice(ROWS * g, ROWS * (g + 1))
-            both = jnp.where(lane < 96, den_high[rows], den_low[rows])
+            both = jnp.where(lane == row, den_high[rows], 0.0) + jnp.where(lane == row + ROWS, den_low[rows], 0.0)
+            both = jnp.broadcast_to(jnp.sum(both, axis=0, keepdims=True), (8, 128))
             for t in range(2):
-                v = num[rows, 128 * t:128 * (t + 1)]
-                base = 4 * (2 * h + g) + 2 * t
-                num_out[base] = jnp.where(lane < 64, v, both).astype(BF16)
-                num_out[base + 1] = jnp.where(lane < 64, pltpu.roll(v, 64, 1), both).astype(BF16)
-
-    @pl.loop(0, ny)
+                v = jnp.concatenate([num[rows, 128 * t:128 * (t + 1)], both], axis=0)
+                num_out[2 * (2 * h + g) + t] = v.astype(BF16)
+
+    @pl.loop(1, nx)
     def _(step):
-        to = (j + step) % ny
-        put(num_out.at[to], num_in.at[half, piece], num_send, num_recv, chunk, to)
-
+        to = (i + step) % nx
+        remote(num_out.at[to], num_in.at[i], num_send, num_recv, to, j).start()
+
+    pltpu.make_async_copy(num_out.at[i], num_in.at[i], num_recv).start()
+    if last_step > 2:
+        ring_take(2)
+    take(num_in, num_recv)
+    total = None
+    for p in range(nx):
+        v = num_in[p].astype(F32)
+        total = v if total is None else total + v
+    both = jnp.where((lane == row) | (lane == row + ROWS), total[ROWS:ROWS + 1], 0.0)
+    total = total[0:ROWS] / jnp.sum(both, axis=1, keepdims=True)
+    att_out[0] = total.astype(BF16)
+    for k in range(2):
+        put(att_out.at[0], att_in.at[half], att_send, att_recv, chunk, 2 * i + k)
     for step in range(3, last_step):
         ring_take(step)
-    own_copy.wait()
-
-    take(num_in, num_recv)
+
+    take(att_in, att_recv)
     attended = []
     for part in range(2):
-        total = None
-        for p in range(nx):
-            v = num_in[part, p].astype(F32)
-            total = v if total is None else total + v
-        attended.append(total[:, 0:64] / (total[:, 64:65] + total[:, 96:97]))
+        v = att_in[part].astype(F32)
+        attended.append(jnp.where(j % 2 == 1, pltpu.roll(v, 64, 1), v)[:, 0:64])
     attended = jnp.concatenate(attended, axis=0).astype(BF16)
     ring_take(last_step)
     take(wf_all.at[1 - c], wf_core_recv)
@@ -407,11 +501,14 @@
         scale = lax.rsqrt(jnp.sum(square, axis=1, keepdims=True) / width + EPSILON)
         for t in range(tiles):
             at = slice(MAIN * t, MAIN * (t + 1))
-            row_out[1, :, at] = (mixed[:, at] * scale * gain(2, t)).astype(BF16)
-
-        spread(1, ff_all, ff_send, ff_recv)
-
-    take(ff_all, ff_recv)
+            sums[:, at] = mixed[:, at] * scale * gain(2, t)
+        ff_all[my_block] = sums[...].astype(BF16)
+        spread(ff_all, ff_a_send, ff_a_recv)
+
+    spread_in(ff_all, ff_a_recv)
+    spread_out(ff_all, ff_b_send, ff_b_recv)
+
+    take(ff_all.at[pl.ds(0, blocks - row_blocks)], ff_b_recv)
     for t in range(tiles):
         norm_in[:, MAIN * t:MAIN * (t + 1)] = chunk_tile(ff_all, t).astype(BF16)
     main_x = norm_in[:, 0:nx * MAIN]
@@ -427,18 +524,19 @@
     both = ff_part(4)
     narrow = gelu(both) * pltpu.roll(both, 96, 1)
     lane_chunk = lax.broadcasted_iota(jnp.int32, narrow.shape, 1)
-    hidden.append(jnp.where(lane_chunk < 32, narrow, 0.0).astype(BF16))
-    first_hidden = jnp.concatenate(hidden[0:2], axis=1)
+    narrow = pltpu.roll(jnp.where(lane_chunk < 32, narrow, 0.0), 64, 1)
+    hidden.append(narrow.astype(BF16))
+    places = [DOWN_AT, DOWN_AT + 144, NARROW_AT]
     for p in range(nx):
-        w = wf_all.at[p // ys, p % ys]
-        v = dot(first_hidden, w[DOWN_AT:DOWN_AT + 256, :])
-        v = v + dot(hidden[2][:, 0:32], w[DOWN_AT + 256:DOWN_REST_AT, :])
+        v = None
+        for h, at in zip(hidden, places):
+            term = dot_nt(h, wf_all[p // ys, p % ys, at:at + MAIN, :])
+            v = term if v is None else v + term
         put_partial(1, p, v)
     v = None
-    for n in range(3):
-        at = DOWN_REST_AT + REST * n
-        rest_w = wf_all[:, :, at:at + REST, :].reshape(nx * REST, 128)
-        term = dot_nt(hidden[n], rest_w)
+    for h, at in zip(hidden, places):
+        rest_w = wf_all[:, :, at + MAIN:at + 144, :].reshape(nx * REST, 128)
+        term = dot_nt(h, rest_w)
         v = term if v is None else v + term
     put_rest(1, v)
     send_partial(1, down_in, down_send, down_recv)
@@ -467,10 +565,8 @@
     take(last_in, last_recv)
     out_ref[...] = last_in[...]
 
-    home = chunk == i
-    take_sent(x_in, 4, x_send, home & is_owner & (my_block // 4 == half))
-    if ys > 1:
-        take(wa_all.at[c, pl.ds(0, ys - 1)], wa_send)
+    take_sent(x_in, 4, x_send, own_rows)
+    take(wa_all.at[c, pl.ds(0, ys - 1)], wa_send)
     take(wa_all.at[c], wa_core_send)
     for step in range(1, last_step + 1):
         for side in range(2):
@@ -478,14 +574,17 @@
             take(wf_all.at[0, 0, rows], ring_send.at[2 * step - 2 + side])
     take(wf_all.at[c], wf_core_send)
     take_sent(qkv_in, ny, qkv_send, home)
-    take_sent(num_out, ny, num_send, home)
+    take(num_out.at[pl.ds(0, nx - 1)], num_send)
+    take_sent(att_in, 2, att_send, home & (j // 2 == i))
     take_sent(row_all, blocks, part_send, is_owner)
     take_sent(ff_all, blocks, down_send, is_owner)
+    take(row_all.at[pl.ds(0, (zs - 1) * row_blocks)], row_b_send)
+    take(ff_all.at[pl.ds(0, (zs - 1) * row_blocks)], ff_b_send)
 
     @pl.when(is_owner)
     def _():
-        take(part_in.at[pl.ds(0, ny - 1)], row_send)
-        take(down_in.at[pl.ds(0, ny - 1)], ff_send)
+        take(row_all.at[pl.ds(0, 3)], row_a_send)
+        take(ff_all.at[pl.ds(0, 3)], ff_a_send)
         take_sent(x_in, nx, last_send, home & (my_block // 4 == half))
 
 
@@ -500,63 +599,61 @@
     ys = nx // 2
     last_step = ys // 2
 
-    x = jnp.pad(inputs.reshape(ROWS // 8, 8, columns), ((0, 0), (0, 0), (0, 256 - columns)))
-    gains = 1.0 + norm_gains
-    gains = jnp.concatenate([gains[:, 0:MAIN], jnp.pad(gains[:, MAIN:], ((0, 0), (0, MAIN - REST)))], axis=0)
-    high = lax.reduce_precision(gains, 8, 7)
-    qkv_weights = jnp.concatenate([w_query, w_key, w_value], axis=1)
-    wa = jnp.concatenate([qkv_weights, high.astype(BF16), (gains - high).astype(BF16)], axis=0)
-    narrow = jnp.pad(jnp.concatenate([w_gate[:, 256:], w_up[:, 256:]], axis=1), ((0, 0), (0, 64)))
-    out_rest = jnp.pad(w_out[:, MAIN:].T, ((0, 0), (0, 64)))
-    down_rest = jnp.pad(w_down[:, MAIN:].T, ((0, 0), (0, 96)))
-    wf = jnp.concatenate(
-        [w_out[:, 0:MAIN], out_rest]
-        + [w_gate[:, 0:128], w_gate[:, 128:256], w_up[:, 0:128], w_up[:, 128:256], narrow]
-        + [w_down[:, 0:MAIN]] + [down_rest[:, 128 * n:128 * (n + 1)] for n in range(3)],
-        axis=0,
-    )
     frequency = ROPE_BASE ** (-jnp.arange(128, dtype=F32) * 2.0 / HEAD_DIM)
     positions = lengths[0] + jnp.arange(STEPS, dtype=jnp.int32)
     angles = positions[:, None].astype(F32) * frequency
     trig = jnp.tile(jnp.stack([jnp.cos(angles), jnp.sin(angles)]), (1, BEAM, 1))
 
+    arrays = (
+        inputs, cache_pool, lengths, block_table, parents, norm_gains,
+        w_query.T, w_key.T, w_value.T, w_out, w_gate, w_up, w_down.T, trig,
+    )
     vmem = pl.BlockSpec(memory_space=pltpu.VMEM)
+    specs = [pl.BlockSpec(memory_space=pltpu.HBM) for _ in arrays]
+    specs[2] = pl.BlockSpec(memory_space=pltpu.SMEM)
+    specs[13] = vmem
     dma = pltpu.SemaphoreType.DMA
+
+    def held(*shape, dtype=BF16):
+        return pltpu.VMEM(shape, dtype)
+
     out = pl.pallas_call(
         functools.partial(layer_kernel, nx, ny, nx * columns),
         name="layer",
         out_shape=jax.ShapeDtypeStruct((4, 8, 256), BF16),
-        in_specs=[vmem, vmem, vmem, pl.BlockSpec(memory_space=pl.ANY), vmem, vmem, vmem, vmem],
+        in_specs=specs,
         out_specs=vmem,
-        scratch_shapes=[
-            pltpu.VMEM((2, ys, A_ROWS, 128), BF16),
-            pltpu.VMEM((2, ys, F_ROWS, 128), BF16),
-            pltpu.VMEM((nx, 8, 128), F32),
-            pltpu.VMEM((rest_tiles, 8, 128), F32),
-            pltpu.VMEM((nx, 8, 256), BF16),
-            pltpu.VMEM((8, span), F32),
-            pltpu.VMEM((2, 8, span), BF16),
-            pltpu.VMEM((8, 8, span), BF16),
-            pltpu.VMEM((8, 8, span), BF16),
-            pltpu.VMEM((64, span), BF16),
-            pltpu.VMEM((2, ROWS, 128), BF16),
-            pltpu.VMEM((ny, ROWS, 128), BF16),
-            pltpu.VMEM(cache_pool.shape, BF16),
-            pltpu.VMEM((ny, ROWS, 128), BF16),
-            pltpu.VMEM((2, nx, ROWS, 128), BF16),
-            pltpu.VMEM((2, 8, 8, span), BF16),
-            pltpu.VMEM((ny, 8, span), BF16),
-            pltpu.VMEM((ny, 8, span), BF16),
-            pltpu.VMEM((nx, 8, 256), BF16),
-            pltpu.VMEM((4, 8, 256), BF16),
-            pltpu.VMEM((8, span), F32),
-            pltpu.VMEM((8, span), F32),
+        scratch_shapes=[pltpu.VMEM(arrays[k].shape, arrays[k].dtype) for k in (0, 1, 3, 4, 5, 6, 7, 8, 9, 10, 11, 12)]
+        + [
+            held(2, ys, A_ROWS, 128),
+            held(2, ys, F_ROWS, 128),
+            held(nx, 8, 128, dtype=F32),
+            held(rest_tiles, 8, 128, dtype=F32),
+            held(4, 8, 256),
+            held(nx, 8, 256),
+            held(8, span, dtype=F32),
+            held(8, 8, span),
+            held(8, 8, span),
+            held(64, span),
+            held(2, ROWS, 128),
+            held(ny, ROWS, 128),
+            held(nx, DEN_ROWS, 128),
+            held(nx, DEN_ROWS, 128),
+            held(1, ROWS, 128),
+            held(2, ROWS, 128),
+            held(2, 8, 8, span),
+            held(ny, 8, span),
+            held(ny, 8, span),
+            held(nx, 8, 256),
+            held(4, 8, 256),
+            held(8, span, dtype=F32),
+            held(8, span, dtype=F32),
         ]
-        + [dma(())] * 5
+        + [dma((12,))] + [dma(())] * 4
         + [dma((2 * last_step,)), dma((2 * last_step,))]
-        + [dma(())] * 19,
-        compiler_params=pltpu.CompilerParams(has_side_effects=True, vmem_limit_bytes=40 << 20),
-    )(x, wa, wf, cache_pool, trig, block_table, lengths.reshape(1, 1), parents)
+        + [dma(())] * 24,
+        compiler_params=pltpu.CompilerParams(collective_id=0, has_side_effects=True, vmem_limit_bytes=60 << 20),
+    )(*arrays)
     return out[:, :, 0:columns].reshape(inputs.shape)
 
 

time: 151 us -> 111 us (0.74)
  the two profiles are of different devices: /device:TPU:69 before, /device:TPU:5 now
where the time goes in v2:
time: 111 us
  Pallas kernels  108 us (97%)
  local copies, waits for them, and re-layouts  1.96 us (2%)
    pallas_call x1, Pallas kernels, body(): pl.pallas_call(functools.partial(layer_kernel, nx, ny, nx * columns), nam...  108 us

profile of v2, /device:TPU:5, one launch (start us, length us, event | category | flops | bytes accessed | tf_op | source)
XLA Modules:
  0.0 111.1 jit_solution(18304487774874693837)
XLA Ops:
  0.7 0.1 multiply_cosine_fusion
  0.8 0.6 tile.4
  1.4 108.4 %layer.1 = bf16[4,8,256]{2,1,0:T(8,128)(2,1)} custom-call(bf16[8,4,144]{2,1,0:T(4,128)(2,1)} %inputs_ref.1, bf16[2,4,128,1024]{3,2,1,0:T(8,128)(2,1)} %cache_ref.1, s32[1]{0:T(128)} %copy.14.length_ref, s32[1,33]{1,0:T(1,128)} %table_ref.1, s32[3,8]{1,0:T(4,128)} %parents_ref.1, f32[4,144]{1,0:T(4,128)} %gains_ref.1, bf16[64,144]{1,0:T(8,128)(2,1)} %bitcast.11, ...), custom_call_target="tpu_custom_call" | custom-call | tf_op jit(solution)/shard_map/layer/pallas_call | solution.py:620
  109.8 1.3 %reshape.108 = bf16[8,4,144]{2,1,0:T(4,128)(2,1)} reshape(bf16[4,8,144]{2,1,0:T(8,128)(2,1)} %bitcast.10) | data formatting | bytes 18432 | tf_op jit(solution)/shard_map/reshape | solution.py:657
  (3 shorter events, 0.0 us)

commit v3 on v2

--- a/solution.py
+++ b/solution.py
@@ -28,11 +28,12 @@
 A_ROWS = 160
 OUT_AT = 0
 OUT_REST_AT = 64
-GATE_AT = 80
-NARROW_AT = 656
-DOWN_AT = 800
-F_ROWS = 1088
-CUT = 544
+B_ROWS = 80
+GATE_AT = 0
+NARROW_AT = 576
+DOWN_AT = 720
+F_ROWS = 1008
+CUT = 512
 DEN_ROWS = 40
 
 
@@ -59,13 +60,14 @@
     out_ref,
     inputs_vm, cache, table_vm, parents_vm, gains_vm,
     wq_vm, wk_vm, wv_vm, wo_vm, wg_vm, wu_vm, wd_vm,
-    wa_all, wf_all, gain_main, gain_rest, x_out, x_in, x_own, row_all, ff_all, norm_in,
-    qkv_out, qkv_in, num_out, num_in, att_out, att_in, part_out, part_in, down_in, last_out, last_in,
-    mixed, sums,
+    wa_all, wb_all, wf_all, gain_main, gain_rest, x_out, x_in, x_own, row_all, ff_all, norm_in,
+    q_out, kv_out, q_in, kv_in, tail_num, tail_den, num_out, num_in, att_out, att_in, part_out,
+    part_z, down_z, sum_out, part_x, down_x, last_out, last_in, mixed, sums,
     load_sem, wa_send, wa_recv, wa_core_send, wa_core_recv, ring_send, ring_recv, wf_core_send, wf_core_recv,
-    x_send, x_recv, row_a_send, row_a_recv, row_b_send, row_b_recv, qkv_send, qkv_recv, num_send, num_recv,
-    att_send, att_recv, part_send, part_recv, ff_a_send, ff_a_recv, ff_b_send, ff_b_recv,
-    down_send, down_recv, last_send, last_recv,
+    wb_send, wb_recv, wb_core_send, wb_core_recv,
+    x_send, x_recv, row_send, row_recv, q_send, q_recv, kv_send, kv_recv, num_send, num_recv,
+    att_send, att_recv, part_send, part_recv, part_x_send, part_x_recv, ff_send, ff_recv,
+    down_send, down_recv, down_x_send, down_x_recv, last_send, last_recv,
 ):
     ys = nx // 2
     zs = ny // 4
@@ -87,15 +89,11 @@
         x_r = 2 * part + c
         return ((y + 8 * ys - 2 * x_r) % ys) * 4 + x_r
 
-    def owner_of(core, block):
-        return 4 * block + 2 * core + block % 2 if zs == 8 else block
-
-    if zs == 8:
-        is_owner = (xj // 2 == c) & (xj % 2 == zj % 2)
-        my_block = zj
-    else:
-        is_owner = j >= 0
-        my_block = j
+    first_block = row_blocks * zj
+    my_part = first_block // 4
+    home = chunk == i
+    own_rows = home & (my_part == half)
+    tail_stride = nx // kv_heads
 
     def remote(src, dst, send_sem, recv_sem, tx, ty):
         return pltpu.make_async_remote_copy(
@@ -117,10 +115,10 @@
     def take(ref, sem):
         pltpu.make_async_copy(ref, ref, sem).wait()
 
-    def take_sent(ref, count, sem, own):
+    def take_sent(ref, count, sem, own, fewer=1):
         @pl.when(own)
         def _():
-            take(ref.at[pl.ds(0, count - 1)], sem)
+            take(ref.at[pl.ds(0, count - fewer)], sem)
 
         @pl.when(jnp.logical_not(own))
         def _():
@@ -137,8 +135,6 @@
     for load in loads:
         load.start()
 
-    home = chunk == i
-    own_rows = home & is_owner & (my_block // 4 == half)
     barrier = pltpu.get_barrier_semaphore()
 
     def hello(tx, ty):
@@ -149,26 +145,15 @@
     hello(sibling, j)
     for step in range(1, zs):
         hello(i, 4 * ((zj + step) % zs) + xj)
-    for step in range(1, 4):
-        if zs == 8:
-            @pl.when((2 * c + zj % 2) == (xj + step) % 4)
-            def _():
-                hello(i, 4 * zj + (xj + step) % 4)
-        else:
-            hello(i, 4 * zj + (xj + step) % 4)
-
-    @pl.when(is_owner)
-    def _():
-        group = group_of(my_block // 4)
-
-        @pl.loop(0, nx)
-        def _(to):
-            @pl.when(jnp.logical_not((to == i) & (group == j)))
-            def _():
-                hello(to, group)
-
-    waits = ys + (zs - 1) + 4
-    waits = waits + jnp.where(is_owner, 3, 0) - jnp.where(own_rows, 1, 0)
+    group = group_of(my_part)
+
+    @pl.loop(0, nx)
+    def _(to):
+        @pl.when(jnp.logical_not((to == i) & (group == j)))
+        def _():
+            hello(to, group)
+
+    waits = ys + (zs - 1) + 16 // row_blocks - jnp.where(own_rows, 1, 0)
 
     loads[0].wait()
     for q in range(4):
@@ -176,9 +161,13 @@
         v = jnp.concatenate([v, jnp.zeros((8, MAIN - REST), F32)], axis=1)
         x_out[q] = v.astype(BF16)
     pl.semaphore_wait(barrier, waits)
-    core_of_chunk = chunk % 2
     for q in range(4):
-        put(x_out.at[q], x_in.at[piece], x_send, x_recv, chunk, owner_of(core_of_chunk, half * 4 + q))
+        block = half * 4 + q
+        for step in range(4):
+            put(
+                x_out.at[q], x_in.at[block % row_blocks, piece], x_send, x_recv,
+                chunk, 4 * (block // row_blocks) + (xj + step) % 4,
+            )
     for load in loads[1:5]:
         load.wait()
     v = jnp.concatenate([wq_vm[...].astype(F32), wk_vm[...].astype(F32), wv_vm[...].astype(F32)], axis=0)
@@ -240,45 +229,32 @@
         return out
 
     def spread(ref, send_sem, recv_sem):
-        for step in range(1, 4):
-            src = ref.at[my_block]
-            remote(src, src, send_sem, recv_sem, i, 4 * zj + (xj + step) % 4).start()
-
-    def spread_in(ref, recv_sem):
-        @pl.when(jnp.logical_not(is_owner))
-        def _():
-            take(ref.at[pl.ds(0, row_blocks)], recv_sem)
-
-        if row_blocks > 1:
-            @pl.when(is_owner)
-            def _():
-                take(ref.at[pl.ds(0, row_blocks - 1)], recv_sem)
-
-    def spread_out(ref, send_sem, recv_sem):
-        src = ref.at[pl.ds(row_blocks * zj, row_blocks)]
+        src = ref.at[pl.ds(first_block, row_blocks)]
         for step in range(1, zs):
             remote(src, src, send_sem, recv_sem, i, 4 * ((zj + step) % zs) + xj).start()
 
-    @pl.when(is_owner)
-    def _():
-        take(x_in, x_recv)
+    take(x_in, x_recv)
+    for b in range(row_blocks):
         rests = []
         for p in range(nx):
-            v = x_in[p].astype(F32)
-            x_own[:, MAIN * p:MAIN * (p + 1)] = v[:, 0:MAIN]
+            v = x_in[b, p].astype(F32)
+            x_own[b, :, MAIN * p:MAIN * (p + 1)] = v[:, 0:MAIN]
             rests.append(v[:, MAIN:2 * MAIN])
         for t, v in enumerate(rest_sum(rests)):
-            x_own[:, MAIN * (nx + t):MAIN * (nx + t + 1)] = v
-        row_all[my_block] = x_own[...].astype(BF16)
-        spread(row_all, row_a_send, row_a_recv)
+            x_own[b, :, MAIN * (nx + t):MAIN * (nx + t + 1)] = v
+        row_all[first_block + b] = x_own[b].astype(BF16)
+    spread(row_all, row_send, row_recv)
 
     for load in loads[5:9]:
         load.wait()
-    own_f = wf_all.at[c, y]
-    own_f[OUT_AT:OUT_REST_AT, :] = wo_vm[:, 0:MAIN]
+    own_b = wb_all.at[c, y]
+    own_b[OUT_AT:OUT_REST_AT, :] = wo_vm[:, 0:MAIN]
     v = jnp.concatenate([wo_vm[:, MAIN:].astype(F32), jnp.zeros((64, MAIN - REST), F32)], axis=1)
     v = jnp.concatenate([v, jnp.zeros((64, MAIN), F32)], axis=0).T
-    own_f[OUT_REST_AT:GATE_AT, :] = v[0:REST].astype(BF16)
+    own_b[OUT_REST_AT:B_ROWS, :] = v[0:REST].astype(BF16)
+    for step in range(1, ys):
+        remote(own_b, own_b, wb_send, wb_recv, 2 * ((y + step) % ys) + c, j).start()
+    own_f = wf_all.at[c, y]
     for n in range(2):
         at = slice(MAIN * n, MAIN * (n + 1))
         own_f[GATE_AT + 144 * n:GATE_AT + 144 * (n + 1), :] = wg_vm[:, at]
@@ -288,9 +264,6 @@
     own_f[NARROW_AT:DOWN_AT, :] = jnp.concatenate(v, axis=1).astype(BF16)
     ring_start(1)
     to_sibling(y)
-
-    spread_in(row_all, row_a_recv)
-    spread_out(row_all, row_b_send, row_b_recv)
 
     take(wa_all.at[c, pl.ds(0, ys - 1)], wa_recv)
     remote(wa_all.at[c], wa_all.at[c], wa_core_send, wa_core_recv, sibling, j).start()
@@ -309,7 +282,7 @@
             return gain_main[t, which:which + 1, :]
         return gain_rest[t - nx, 4 + which:5 + which, :]
 
-    take(row_all.at[pl.ds(0, blocks - row_blocks)], row_b_recv)
+    take(row_all.at[pl.ds(0, blocks - row_blocks)], row_recv)
 
     def chunk_tile(ref, t):
         at = slice(MAIN * t, MAIN * (t + 1))
@@ -326,17 +299,22 @@
     main_w = wa_all[:, :, 0:MAIN, :].reshape(nx * MAIN, 128)
     rest_w = wa_all[:, :, MAIN:QKV_ROWS, :].reshape(nx * REST, 128)
     qkv = dot(norm_in[:, 0:nx * MAIN], main_w) + dot(norm_in[:, nx * MAIN:nx * MAIN + nx * REST], rest_w)
-    qkv = qkv.astype(BF16)
-    qkv_out[0] = qkv[0:ROWS]
-    qkv_out[1] = qkv[ROWS:2 * ROWS]
-
+    lane_half = lax.broadcasted_iota(jnp.int32, (ROWS // 2, 128), 1) < 64
+    for part in range(2):
+        first, second = qkv[ROWS * part:ROWS * part + 16], qkv[ROWS * part + 16:ROWS * (part + 1)]
+        q_out[part] = jnp.where(lane_half, first, pltpu.roll(second, 64, 1)).astype(BF16)
+        kv_out[part] = jnp.where(lane_half, pltpu.roll(first, 64, 1), second).astype(BF16)
+    for part in range(2):
+        put(kv_out.at[part], kv_in.at[j % 8], kv_send, kv_recv, tail_stride * (j // 8), group_of(part))
     for part in range(2):
         group = group_of(part)
 
         @pl.loop(0, nx)
         def _(step):
-            put(qkv_out.at[part], qkv_in.at[j], qkv_send, qkv_recv, (i + step) % nx, group)
-
+            put(q_out.at[part], q_in.at[j], q_send, q_recv, (i + step) % nx, group)
+
+    take(wb_all.at[c, pl.ds(0, ys - 1)], wb_recv)
+    remote(wb_all.at[c], wb_all.at[c], wb_core_send, wb_core_recv, sibling, j).start()
     if last_step > 1:
         ring_take(1)
 
@@ -372,20 +350,25 @@
             chosen = jnp.where(beam_lane == current, parents_vm[at - 1:at, :].astype(F32), 0.0)
             parent = jnp.sum(chosen, axis=1, keepdims=True).astype(jnp.int32)
             current = jnp.where(row_step >= at, parent, current)
-    tail = jnp.where(i == 0, tail, 0.0)
     tail_mask = jnp.concatenate([tail, tail], axis=0) > 0.5
 
     cosine, sine = trig_ref[0], trig_ref[1]
-    take(qkv_in, qkv_recv)
-
-    def quarter(source, at, parts):
-        span = 128 // parts
+    take(q_in, q_recv)
+
+    def query_tile(at):
+        first, second = q_in[at].astype(F32), q_in[at + 1].astype(F32)
+        upper = jnp.where(lane_half, first, pltpu.roll(second, 64, 1))
+        lower = jnp.where(lane_half, pltpu.roll(first, 64, 1), second)
+        return jnp.concatenate([upper, lower], axis=0)
+
+    def kv_tile(source, at):
         total = None
-        for m in range(parts):
-            v = qkv_in[source + m].astype(F32)
-            shift = (span * m - at) % 128
+        for m in range(4):
+            v = kv_in[source + m].astype(F32)
+            v = jnp.concatenate([v, pltpu.roll(v, 64, 1)], axis=0)
+            shift = (32 * m - at) % 128
             v = pltpu.roll(v, shift, 1) if shift else v
-            total = v if total is None else jnp.where(lane >= span * m, v, total)
+            total = v if total is None else jnp.where(lane >= 32 * m, v, total)
         return total
 
     def rotated(u, w):
@@ -394,18 +377,30 @@
     def wide(u, w):
         return jnp.concatenate([u, w], axis=1)
 
-    for h in range(kv_heads):
+    def query_of(h):
         qs = []
         for g in range(2):
             base = 4 * (2 * h + g)
-            u, w = rotated(quarter(base, 0, 2), quarter(base + 2, 0, 2))
-            qs.append(wide(u, w) * HEAD_DIM ** -0.5)
-        query = jnp.concatenate(qs, axis=0).astype(BF16)
-        key = wide(*rotated(quarter(8 * h, 64, 4), quarter(8 * h + 4, 64, 4))).astype(BF16)
-        value = wide(quarter(8 * h, 96, 4), quarter(8 * h + 4, 96, 4)).astype(BF16)
-        weights = jnp.where(tail_mask, capped(dot_nt(query, key)), 0.0)
-        den = jnp.sum(weights, axis=1, keepdims=True)
-        num = dot(weights.astype(BF16), value)
+            qs.append(wide(*rotated(query_tile(base), query_tile(base + 2))) * HEAD_DIM ** -0.5)
+        return jnp.concatenate(qs, axis=0).astype(BF16)
+
+    tail_num[...] = jnp.zeros(tail_num.shape, F32)
+    tail_den[...] = jnp.zeros(tail_den.shape, F32)
+
+    @pl.when(i % tail_stride == 0)
+    def _():
+        h = i // tail_stride
+        take(kv_in, kv_recv)
+        key = wide(*rotated(kv_tile(0, 0), kv_tile(4, 0))).astype(BF16)
+        value = wide(kv_tile(0, 32), kv_tile(4, 32)).astype(BF16)
+        weights = jnp.where(tail_mask, capped(dot_nt(query_of(h), key)), 0.0)
+        tail_den[h] = jnp.broadcast_to(jnp.sum(weights, axis=1, keepdims=True), (2 * ROWS, 128))
+        tail_num[h] = dot(weights.astype(BF16), value)
+
+    for h in range(kv_heads):
+        query = query_of(h)
+        den = tail_den[h, :, 0:1]
+        num = tail_num[h]
         for slot in range(4):
             at = slice(HEAD_DIM * h, HEAD_DIM * (h + 1))
             weights = jnp.where(masks[slot], capped(dot_nt(query, cache[0, slot, :, at])), 0.0)
@@ -439,8 +434,6 @@
     att_out[0] = total.astype(BF16)
     for k in range(2):
         put(att_out.at[0], att_in.at[half], att_send, att_recv, chunk, 2 * i + k)
-    for step in range(3, last_step):
-        ring_take(step)
 
     take(att_in, att_recv)
     attended = []
@@ -448,8 +441,7 @@
         v = att_in[part].astype(F32)
         attended.append(jnp.where(j % 2 == 1, pltpu.roll(v, 64, 1), v)[:, 0:64])
     attended = jnp.concatenate(attended, axis=0).astype(BF16)
-    ring_take(last_step)
-    take(wf_all.at[1 - c], wf_core_recv)
+    take(wb_all.at[1 - c], wb_core_recv)
 
     def put_partial(which, t, v):
         for k in range(blocks):
@@ -462,53 +454,65 @@
             put_partial(which, nx + t, v[:, 128 * t:128 * (t + 1)])
 
     for p in range(nx):
-        put_partial(0, p, dot(attended, wf_all[p // ys, p % ys, OUT_AT:OUT_REST_AT, :]))
-    rest_w = wf_all[:, :, OUT_REST_AT:GATE_AT, :].reshape(nx * REST, 128)
+        put_partial(0, p, dot(attended, wb_all[p // ys, p % ys, OUT_AT:OUT_REST_AT, :]))
+    rest_w = wb_all[:, :, OUT_REST_AT:B_ROWS, :].reshape(nx * REST, 128)
     put_rest(0, dot_nt(attended, rest_w[:, 0:64]))
 
     def send_partial(which, dst_all, send_sem, recv_sem):
-        @pl.loop(0, blocks)
-        def _(k):
-            put(part_out.at[which, k], dst_all.at[j], send_sem, recv_sem, i, owner_of(c, k))
-
-    def add_up(ref, t):
-        total = None
-        for s in range(ny):
-            v = ref[s, :, MAIN * t:MAIN * (t + 1)].astype(F32)
-            total = v if total is None else total + v
-        return total
-
-    def add_rows(ref):
-        square = None
-        for t in range(tiles):
-            v = add_up(ref, t)
-            sums[:, MAIN * t:MAIN * (t + 1)] = v
-            square = v * v if square is None else square + v * v
-        return lax.rsqrt(jnp.sum(square, axis=1, keepdims=True) / width + EPSILON)
-
-    send_partial(0, part_in, part_send, part_recv)
-
-    @pl.when(is_owner)
-    def _():
-        take(part_in, part_recv)
-        scale = add_rows(part_in)
+        for step in range(1, zs):
+            to = (zj + step) % zs
+            src = part_out.at[which, pl.ds(row_blocks * to, row_blocks)]
+            remote(src, dst_all.at[step - 1], send_sem, recv_sem, i, 4 * to + xj).start()
+
+    def add_z(which, ref, dst_all, send_sem, recv_sem):
+        for b in range(row_blocks):
+            for t in range(tiles):
+                at = slice(MAIN * t, MAIN * (t + 1))
+                total = part_out[which, first_block + b, :, at].astype(F32)
+                for s in range(zs - 1):
+                    total = total + ref[s, b, :, at].astype(F32)
+                sums[b, :, at] = total
+            sum_out[which, b] = sums[b].astype(BF16)
+        for step in range(1, 4):
+            remote(
+                sum_out.at[which], dst_all.at[step - 1], send_sem, recv_sem, i, 4 * zj + (xj + step) % 4
+            ).start()
+
+    def add_x(ref, b):
         square = None
         for t in range(tiles):
             at = slice(MAIN * t, MAIN * (t + 1))
-            v = x_own[:, at] + sums[:, at] * scale * gain(1, t)
-            mixed[:, at] = v
+            v = sums[b, :, at]
+            for s in range(3):
+                v = v + ref[s, b, :, at].astype(F32)
+            sums[b, :, at] = v
+            square = v * v if square is None else square + v * v
+        return lax.rsqrt(jnp.sum(square, axis=1, keepdims=True) / width + EPSILON)
+
+    send_partial(0, part_z, part_send, part_recv)
+    take(part_z, part_recv)
+    add_z(0, part_z, part_x, part_x_send, part_x_recv)
+    for step in range(3, last_step):
+        ring_take(step)
+    take(part_x, part_x_recv)
+    for b in range(row_blocks):
+        scale = add_x(part_x, b)
+        square = None
+        for t in range(tiles):
+            at = slice(MAIN * t, MAIN * (t + 1))
+            v = x_own[b, :, at] + sums[b, :, at] * scale * gain(1, t)
+            mixed[b, :, at] = v
             square = v * v if square is None else square + v * v
         scale = lax.rsqrt(jnp.sum(square, axis=1, keepdims=True) / width + EPSILON)
         for t in range(tiles):
             at = slice(MAIN * t, MAIN * (t + 1))
-            sums[:, at] = mixed[:, at] * scale * gain(2, t)
-        ff_all[my_block] = sums[...].astype(BF16)
-        spread(ff_all, ff_a_send, ff_a_recv)
-
-    spread_in(ff_all, ff_a_recv)
-    spread_out(ff_all, ff_b_send, ff_b_recv)
-
-    take(ff_all.at[pl.ds(0, blocks - row_blocks)], ff_b_recv)
+            sums[b, :, at] = mixed[b, :, at] * scale * gain(2, t)
+        ff_all[first_block + b] = sums[b].astype(BF16)
+    spread(ff_all, ff_send, ff_recv)
+    ring_take(last_step)
+    take(wf_all.at[1 - c], wf_core_recv)
+
+    take(ff_all.at[pl.ds(0, blocks - row_blocks)], ff_recv)
     for t in range(tiles):
         norm_in[:, MAIN * t:MAIN * (t + 1)] = chunk_tile(ff_all, t).astype(BF16)
     main_x = norm_in[:, 0:nx * MAIN]
@@ -539,53 +543,57 @@
         term = dot_nt(h, rest_w)
         v = term if v is None else v + term
     put_rest(1, v)
-    send_partial(1, down_in, down_send, down_recv)
-
-    @pl.when(is_owner)
-    def _():
-        take(down_in, down_recv)
-        scale = add_rows(down_in)
+    send_partial(1, down_z, down_send, down_recv)
+    take(down_z, down_recv)
+    add_z(1, down_z, down_x, down_x_send, down_x_recv)
+    take(down_x, down_x_recv)
+
+    share = nx // 4
+    for b in range(row_blocks):
+        scale = add_x(down_x, b)
 
         def result(t):
             at = slice(MAIN * t, MAIN * (t + 1))
-            return mixed[:, at] + sums[:, at] * scale * gain(3, t)
+            return mixed[b, :, at] + sums[b, :, at] * scale * gain(3, t)
 
         for p in range(nx):
             v = result(nx + p // 8)
             shift = (128 - REST * (p % 8)) % 128
             v = pltpu.roll(v, shift, 1) if shift else v
-            last_out[p] = jnp.concatenate([result(p), v], axis=1).astype(BF16)
-        group = group_of(my_block // 4)
-
-        @pl.loop(0, nx)
-        def _(p):
+            last_out[b, p] = jnp.concatenate([result(p), v], axis=1).astype(BF16)
+        for m in range(share):
+            p = share * xj + m
             to = 2 * (p % ys) + p // ys
-            put(last_out.at[p], last_in.at[my_block % 4], last_send, last_recv, to, group)
+            put(
+                last_out.at[b, p], last_in.at[(first_block + b) % 4], last_send, last_recv,
+                to, group_of(my_part),
+            )
 
     take(last_in, last_recv)
     out_ref[...] = last_in[...]
 
-    take_sent(x_in, 4, x_send, own_rows)
+    x_sent = last_out.at[0]
+    take_sent(x_sent, 16, x_send, own_rows, row_blocks)
     take(wa_all.at[c, pl.ds(0, ys - 1)], wa_send)
     take(wa_all.at[c], wa_core_send)
+    take(wb_all.at[c, pl.ds(0, ys - 1)], wb_send)
+    take(wb_all.at[c], wb_core_send)
     for step in range(1, last_step + 1):
         for side in range(2):
             rows = pl.ds(0, F_ROWS) if step < last_step else pl.ds(CUT * side, F_ROWS - CUT if side else CUT)
             take(wf_all.at[0, 0, rows], ring_send.at[2 * step - 2 + side])
     take(wf_all.at[c], wf_core_send)
-    take_sent(qkv_in, ny, qkv_send, home)
+    take_sent(q_in, ny, q_send, home)
+    take_sent(kv_out, 2, kv_send, home & (i == tail_stride * (j // 8)))
     take(num_out.at[pl.ds(0, nx - 1)], num_send)
     take_sent(att_in, 2, att_send, home & (j // 2 == i))
-    take_sent(row_all, blocks, part_send, is_owner)
-    take_sent(ff_all, blocks, down_send, is_owner)
-    take(row_all.at[pl.ds(0, (zs - 1) * row_blocks)], row_b_send)
-    take(ff_all.at[pl.ds(0, (zs - 1) * row_blocks)], ff_b_send)
-
-    @pl.when(is_owner)
-    def _():
-        take(row_all.at[pl.ds(0, 3)], row_a_send)
-        take(ff_all.at[pl.ds(0, 3)], ff_a_send)
-        take_sent(x_in, nx, last_send, home & (my_block // 4 == half))
+    take(row_all.at[pl.ds(0, (zs - 1) * row_blocks)], row_send)
+    take(ff_all.at[pl.ds(0, (zs - 1) * row_blocks)], ff_send)
+    take(part_z, part_send)
+    take(down_z, down_send)
+    take(part_x, part_x_send)
+    take(down_x, down_x_send)
+    take_sent(x_sent, row_blocks * share, last_send, own_rows & (piece // share == xj), row_blocks)
 
 
 def body(
@@ -598,6 +606,8 @@
     span = tiles * MAIN
     ys = nx // 2
     last_step = ys // 2
+    zs = ny // 4
+    row_blocks = 8 // zs
 
     frequency = ROPE_BASE ** (-jnp.arange(128, dtype=F32) * 2.0 / HEAD_DIM)
     positions = lengths[0] + jnp.arange(STEPS, dtype=jnp.int32)
@@ -626,32 +636,40 @@
         scratch_shapes=[pltpu.VMEM(arrays[k].shape, arrays[k].dtype) for k in (0, 1, 3, 4, 5, 6, 7, 8, 9, 10, 11, 12)]
         + [
             held(2, ys, A_ROWS, 128),
+            held(2, ys, B_ROWS, 128),
             held(2, ys, F_ROWS, 128),
             held(nx, 8, 128, dtype=F32),
             held(rest_tiles, 8, 128, dtype=F32),
             held(4, 8, 256),
-            held(nx, 8, 256),
-            held(8, span, dtype=F32),
+            held(row_blocks, nx, 8, 256),
+            held(row_blocks, 8, span, dtype=F32),
             held(8, 8, span),
             held(8, 8, span),
             held(64, span),
-            held(2, ROWS, 128),
-            held(ny, ROWS, 128),
+            held(2, ROWS // 2, 128),
+            held(2, ROWS // 2, 128),
+            held(ny, ROWS // 2, 128),
+            held(8, ROWS // 2, 128),
+            held(ny // 8, 2 * ROWS, HEAD_DIM, dtype=F32),
+            held(ny // 8, 2 * ROWS, 128, dtype=F32),
             held(nx, DEN_ROWS, 128),
             held(nx, DEN_ROWS, 128),
             held(1, ROWS, 128),
             held(2, ROWS, 128),
             held(2, 8, 8, span),
-            held(ny, 8, span),
-            held(ny, 8, span),
-            held(nx, 8, 256),
+            held(zs - 1, row_blocks, 8, span),
+            held(zs - 1, row_blocks, 8, span),
+            held(2, row_blocks, 8, span),
+            held(3, row_blocks, 8, span),
+            held(3, row_blocks, 8, span),
+            held(row_blocks, 16, 8, 256),
             held(4, 8, 256),
-            held(8, span, dtype=F32),
-            held(8, span, dtype=F32),
+            held(row_blocks, 8, span, dtype=F32),
+            held(row_blocks, 8, span, dtype=F32),
         ]
         + [dma((12,))] + [dma(())] * 4
         + [dma((2 * last_step,)), dma((2 * last_step,))]
-        + [dma(())] * 24,
+        + [dma(())] * 30,
         compiler_params=pltpu.CompilerParams(collective_id=0, has_side_effects=True, vmem_limit_bytes=60 << 20),
     )(*arrays)
     return out[:, :, 0:columns].reshape(inputs.shape)

time: 111 us -> 110 us (level)
  the two profiles are of different devices: /device:TPU:5 before, /device:TPU:1 now
where the time goes in v3:
time: 110 us; the launch traced here: 109 us
  Pallas kernels  107 us (97%)
  local copies, waits for them, and re-layouts  1.96 us (2%)
    pallas_call x1, Pallas kernels, body(): pl.pallas_call(functools.partial(layer_kernel, nx, ny, nx * columns), nam...  107 us

profile of v3, /device:TPU:1, one launch (start us, length us, event | category | flops | bytes accessed | tf_op | source)
XLA Modules:
  0.0 109.3 jit_solution(13473025100024346907)
XLA Ops:
  0.7 0.1 multiply_cosine_fusion
  0.8 0.6 tile.4
  1.4 106.5 %layer.1 = bf16[4,8,256]{2,1,0:T(8,128)(2,1)} custom-call(bf16[8,4,144]{2,1,0:T(4,128)(2,1)} %inputs_ref.1, bf16[2,4,128,1024]{3,2,1,0:T(8,128)(2,1)} %cache_ref.1, s32[1]{0:T(128)} %copy.14.length_ref, s32[1,33]{1,0:T(1,128)} %table_ref.1, s32[3,8]{1,0:T(4,128)} %parents_ref.1, f32[4,144]{1,0:T(4,128)} %gains_ref.1, bf16[64,144]{1,0:T(8,128)(2,1)} %bitcast.11, ...), custom_call_target="tpu_custom_call" | custom-call | tf_op jit(solution)/shard_map/layer/pallas_call | solution.py:630
  107.9 1.3 %reshape.108 = bf16[8,4,144]{2,1,0:T(4,128)(2,1)} reshape(bf16[4,8,144]{2,1,0:T(8,128)(2,1)} %bitcast.10) | data formatting | bytes 18432 | tf_op jit(solution)/shard_map/reshape | solution.py:675
  (3 shorter events, 0.0 us)

commit v4 on v3

--- a/solution.py
+++ b/solution.py
@@ -65,7 +65,7 @@
     part_z, down_z, sum_out, part_x, down_x, last_out, last_in, mixed, sums,
     load_sem, wa_send, wa_recv, wa_core_send, wa_core_recv, ring_send, ring_recv, wf_core_send, wf_core_recv,
     wb_send, wb_recv, wb_core_send, wb_core_recv,
-    x_send, x_recv, row_send, row_recv, q_send, q_recv, kv_send, kv_recv, num_send, num_recv,
+    x_send, x_recv, x_row_send, x_row_recv, row_send, row_recv, q_send, q_recv, kv_send, kv_recv, num_send, num_recv,
     att_send, att_recv, part_send, part_recv, part_x_send, part_x_recv, ff_send, ff_recv,
     down_send, down_recv, down_x_send, down_x_recv, last_send, last_recv,
 ):
@@ -89,11 +89,17 @@
         x_r = 2 * part + c
         return ((y + 8 * ys - 2 * x_r) % ys) * 4 + x_r
 
-    first_block = row_blocks * zj
+    shift = (y + 8 * ys - 2 * c - 1) % ys if zs == 8 else 0
+    first_block = row_blocks * ((zj + zs - shift) % zs)
+    share = nx // 4
     my_part = first_block // 4
     home = chunk == i
-    own_rows = home & (my_part == half)
+    own_rows = home & (my_part == half) & (piece // share == xj)
     tail_stride = nx // kv_heads
+
+    def row_of(block):
+        there = (chunk // 2 + 8 * ys - 2 * (chunk % 2) - 1) % ys if zs == 8 else 0
+        return (block + there) % zs
 
     def remote(src, dst, send_sem, recv_sem, tx, ty):
         return pltpu.make_async_remote_copy(
@@ -147,13 +153,17 @@
         hello(i, 4 * ((zj + step) % zs) + xj)
     group = group_of(my_part)
 
-    @pl.loop(0, nx)
-    def _(to):
+    for m in range(share):
+        p = share * xj + m
+        to = 2 * (p % ys) + p // ys
+
         @pl.when(jnp.logical_not((to == i) & (group == j)))
         def _():
             hello(to, group)
 
-    waits = ys + (zs - 1) + 16 // row_blocks - jnp.where(own_rows, 1, 0)
+    for step in range(1, 4):
+        hello(i, 4 * zj + (xj + step) % 4)
+    waits = ys + (zs - 1) + 3 + 4 // row_blocks - jnp.where(own_rows, 1, 0)
 
     loads[0].wait()
     for q in range(4):
@@ -163,11 +173,10 @@
     pl.semaphore_wait(barrier, waits)
     for q in range(4):
         block = half * 4 + q
-        for step in range(4):
-            put(
-                x_out.at[q], x_in.at[block % row_blocks, piece], x_send, x_recv,
-                chunk, 4 * (block // row_blocks) + (xj + step) % 4,
-            )
+        put(
+            x_out.at[q], x_in.at[piece, block % row_blocks], x_send, x_recv,
+            chunk, 4 * row_of(block // row_blocks) + piece // share,
+        )
     for load in loads[1:5]:
         load.wait()
     v = jnp.concatenate([wq_vm[...].astype(F32), wk_vm[...].astype(F32), wv_vm[...].astype(F32)], axis=0)
@@ -233,11 +242,15 @@
         for step in range(1, zs):
             remote(src, src, send_sem, recv_sem, i, 4 * ((zj + step) % zs) + xj).start()
 
-    take(x_in, x_recv)
+    quarter = x_in.at[pl.ds(share * xj, share)]
+    take(quarter, x_recv)
+    for step in range(1, 4):
+        remote(quarter, quarter, x_row_send, x_row_recv, i, 4 * zj + (xj + step) % 4).start()
+    take(x_in.at[pl.ds(0, 3 * share)], x_row_recv)
     for b in range(row_blocks):
         rests = []
         for p in range(nx):
-            v = x_in[b, p].astype(F32)
+            v = x_in[p, b].astype(F32)
             x_own[b, :, MAIN * p:MAIN * (p + 1)] = v[:, 0:MAIN]
             rests.append(v[:, MAIN:2 * MAIN])
         for t, v in enumerate(rest_sum(rests)):
@@ -315,9 +328,6 @@
 
     take(wb_all.at[c, pl.ds(0, ys - 1)], wb_recv)
     remote(wb_all.at[c], wb_all.at[c], wb_core_send, wb_core_recv, sibling, j).start()
-    if last_step > 1:
-        ring_take(1)
-
     row = lax.broadcasted_iota(jnp.int32, (ROWS, 1), 0)
     row_step, row_beam = row & 3, jnp.right_shift(row, 2)
     for load in loads[9:12]:
@@ -422,8 +432,6 @@
         remote(num_out.at[to], num_in.at[i], num_send, num_recv, to, j).start()
 
     pltpu.make_async_copy(num_out.at[i], num_in.at[i], num_recv).start()
-    if last_step > 2:
-        ring_take(2)
     take(num_in, num_recv)
     total = None
     for p in range(nx):
@@ -434,6 +442,8 @@
     att_out[0] = total.astype(BF16)
     for k in range(2):
         put(att_out.at[0], att_in.at[half], att_send, att_recv, chunk, 2 * i + k)
+    if last_step > 1:
+        ring_take(1)
 
     take(att_in, att_recv)
     attended = []
@@ -461,7 +471,7 @@
     def send_partial(which, dst_all, send_sem, recv_sem):
         for step in range(1, zs):
             to = (zj + step) % zs
-            src = part_out.at[which, pl.ds(row_blocks * to, row_blocks)]
+            src = part_out.at[which, pl.ds(row_blocks * ((to + zs - shift) % zs), row_blocks)]
             remote(src, dst_all.at[step - 1], send_sem, recv_sem, i, 4 * to + xj).start()
 
     def add_z(which, ref, dst_all, send_sem, recv_sem):
@@ -490,6 +500,8 @@
         return lax.rsqrt(jnp.sum(square, axis=1, keepdims=True) / width + EPSILON)
 
     send_partial(0, part_z, part_send, part_recv)
+    if last_step > 2:
+        ring_take(2)
     take(part_z, part_recv)
     add_z(0, part_z, part_x, part_x_send, part_x_recv)
     for step in range(3, last_step):
@@ -548,7 +560,6 @@
     add_z(1, down_z, down_x, down_x_send, down_x_recv)
     take(down_x, down_x_recv)
 
-    share = nx // 4
     for b in range(row_blocks):
         scale = add_x(down_x, b)
 
@@ -573,7 +584,8 @@
     out_ref[...] = last_in[...]
 
     x_sent = last_out.at[0]
-    take_sent(x_sent, 16, x_send, own_rows, row_blocks)
+    take_sent(x_sent, 4, x_send, own_rows, row_blocks)
+    take(x_in.at[pl.ds(0, 3 * share)], x_row_send)
     take(wa_all.at[c, pl.ds(0, ys - 1)], wa_send)
     take(wa_all.at[c], wa_core_send)
     take(wb_all.at[c, pl.ds(0, ys - 1)], wb_send)
@@ -593,7 +605,7 @@
     take(down_z, down_send)
     take(part_x, part_x_send)
     take(down_x, down_x_send)
-    take_sent(x_sent, row_blocks * share, last_send, own_rows & (piece // share == xj), row_blocks)
+    take_sent(x_sent, row_blocks * share, last_send, own_rows, row_blocks)
 
 
 def body(
@@ -641,7 +653,7 @@
             held(nx, 8, 128, dtype=F32),
             held(rest_tiles, 8, 128, dtype=F32),
             held(4, 8, 256),
-            held(row_blocks, nx, 8, 256),
+            held(nx, row_blocks, 8, 256),
             held(row_blocks, 8, span, dtype=F32),
             held(8, 8, span),
             held(8, 8, span),
@@ -669,7 +681,7 @@
         ]
         + [dma((12,))] + [dma(())] * 4
         + [dma((2 * last_step,)), dma((2 * last_step,))]
-        + [dma(())] * 30,
+        + [dma(())] * 32,
         compiler_params=pltpu.CompilerParams(collective_id=0, has_side_effects=True, vmem_limit_bytes=60 << 20),
     )(*arrays)
     return out[:, :, 0:columns].reshape(inputs.shape)

time: 110 us -> 104 us (0.945)
  Pallas kernels: 107 us -> 101 us
    pallas_call x1, Pallas kernels: 107 us -> 101 us  [body(): pl.pallas_call(functools.partial(layer_kernel, nx, ny, nx * columns), nam...]
where the time goes in v4:
time: 104 us; the launch traced here: 103 us
  Pallas kernels  101 us (97%)
  local copies, waits for them, and re-layouts  1.96 us (2%)
    pallas_call x1, Pallas kernels, body(): pl.pallas_call(functools.partial(layer_kernel, nx, ny, nx * columns), nam...  101 us

profile of v4, /device:TPU:1, one launch (start us, length us, event | category | flops | bytes accessed | tf_op | source)
XLA Modules:
  0.0 103.4 jit_solution(338324920094837621)
XLA Ops:
  0.7 0.1 multiply_cosine_fusion
  0.8 0.6 tile.4
  1.4 100.6 %layer.1 = bf16[4,8,256]{2,1,0:T(8,128)(2,1)} custom-call(bf16[8,4,144]{2,1,0:T(4,128)(2,1)} %inputs_ref.1, bf16[2,4,128,1024]{3,2,1,0:T(8,128)(2,1)} %cache_ref.1, s32[1]{0:T(128)} %copy.14.length_ref, s32[1,33]{1,0:T(1,128)} %table_ref.1, s32[3,8]{1,0:T(4,128)} %parents_ref.1, f32[4,144]{1,0:T(4,128)} %gains_ref.1, bf16[64,144]{1,0:T(8,128)(2,1)} %bitcast.11, ...), custom_call_target="tpu_custom_call" | custom-call | tf_op jit(solution)/shard_map/layer/pallas_call | solution.py:642
  102.1 1.3 %reshape.108 = bf16[8,4,144]{2,1,0:T(4,128)(2,1)} reshape(bf16[4,8,144]{2,1,0:T(8,128)(2,1)} %bitcast.10) | data formatting | bytes 18432 | tf_op jit(solution)/shard_map/reshape | solution.py:687
  (3 shorter events, 0.0 us)

commit v5 on v4

--- a/solution.py
+++ b/solution.py
@@ -56,7 +56,7 @@
 def layer_kernel(
     nx, ny, width,
     inputs_ref, cache_ref, length_ref, table_ref, parents_ref, gains_ref,
-    wq_ref, wk_ref, wv_ref, wo_ref, wg_ref, wu_ref, wd_ref, trig_ref,
+    wq_ref, wk_ref, wv_ref, wo_ref, wg_ref, wu_ref, wd_ref, cosine_ref, sine_ref,
     out_ref,
     inputs_vm, cache, table_vm, parents_vm, gains_vm,
     wq_vm, wk_vm, wv_vm, wo_vm, wg_vm, wu_vm, wd_vm,
@@ -76,6 +76,8 @@
     rest_tiles = tiles - nx
     blocks = 8
     row_blocks = blocks // zs
+    z_steps = sorted(range(1, zs), key=lambda d: -min(d, zs - d))
+    y_steps = sorted(range(1, ys), key=lambda d: -min(d, ys - d))
     i = lax.axis_index("gx")
     j = lax.axis_index("gy")
     y, c = i // 2, i % 2
@@ -188,7 +190,7 @@
     v = jnp.concatenate([v[:, 0:MAIN], v[:, MAIN:]], axis=0)
     high = v.astype(BF16).astype(F32)
     wa_all[c, y, QKV_ROWS:A_ROWS, :] = jnp.concatenate([high, v - high], axis=0).astype(BF16)
-    for step in range(1, ys):
+    for step in y_steps:
         remote(wa_all.at[c, y], wa_all.at[c, y], wa_send, wa_recv, 2 * ((y + step) % ys) + c, j).start()
 
     right = 2 * ((y + 1) % ys) + c
@@ -239,7 +241,7 @@
 
     def spread(ref, send_sem, recv_sem):
         src = ref.at[pl.ds(first_block, row_blocks)]
-        for step in range(1, zs):
+        for step in z_steps:
             remote(src, src, send_sem, recv_sem, i, 4 * ((zj + step) % zs) + xj).start()
 
     quarter = x_in.at[pl.ds(share * xj, share)]
@@ -265,7 +267,7 @@
     v = jnp.concatenate([wo_vm[:, MAIN:].astype(F32), jnp.zeros((64, MAIN - REST), F32)], axis=1)
     v = jnp.concatenate([v, jnp.zeros((64, MAIN), F32)], axis=0).T
     own_b[OUT_REST_AT:B_ROWS, :] = v[0:REST].astype(BF16)
-    for step in range(1, ys):
+    for step in y_steps:
         remote(own_b, own_b, wb_send, wb_recv, 2 * ((y + step) % ys) + c, j).start()
     own_f = wf_all.at[c, y]
     for n in range(2):
@@ -324,7 +326,7 @@
 
         @pl.loop(0, nx)
         def _(step):
-            put(q_out.at[part], q_in.at[j], q_send, q_recv, (i + step) % nx, group)
+            put(q_out.at[part], q_in.at[j], q_send, q_recv, (i + 2 * j + step) % nx, group)
 
     take(wb_all.at[c, pl.ds(0, ys - 1)], wb_recv)
     remote(wb_all.at[c], wb_all.at[c], wb_core_send, wb_core_recv, sibling, j).start()
@@ -362,7 +364,8 @@
             current = jnp.where(row_step >= at, parent, current)
     tail_mask = jnp.concatenate([tail, tail], axis=0) > 0.5
 
-    cosine, sine = trig_ref[0], trig_ref[1]
+    cosine = jnp.concatenate([cosine_ref[...]] * BEAM, axis=0)
+    sine = jnp.concatenate([sine_ref[...]] * BEAM, axis=0)
     take(q_in, q_recv)
 
     def query_tile(at):
@@ -426,10 +429,11 @@
                 v = jnp.concatenate([num[rows, 128 * t:128 * (t + 1)], both], axis=0)
                 num_out[2 * (2 * h + g) + t] = v.astype(BF16)
 
-    @pl.loop(1, nx)
-    def _(step):
-        to = (i + step) % nx
-        remote(num_out.at[to], num_in.at[i], num_send, num_recv, to, j).start()
+    for step in y_steps + [0]:
+        for core in range(2):
+            to = 2 * ((y + step) % ys) + (c + core) % 2
+            if step or core:
+                remote(num_out.at[to], num_in.at[i], num_send, num_recv, to, j).start()
 
     pltpu.make_async_copy(num_out.at[i], num_in.at[i], num_recv).start()
     take(num_in, num_recv)
@@ -469,7 +473,7 @@
     put_rest(0, dot_nt(attended, rest_w[:, 0:64]))
 
     def send_partial(which, dst_all, send_sem, recv_sem):
-        for step in range(1, zs):
+        for step in z_steps:
             to = (zj + step) % zs
             src = part_out.at[which, pl.ds(row_blocks * ((to + zs - shift) % zs), row_blocks)]
             remote(src, dst_all.at[step - 1], send_sem, recv_sem, i, 4 * to + xj).start()
@@ -581,7 +585,10 @@
             )
 
     take(last_in, last_recv)
-    out_ref[...] = last_in[...]
+    for q in range(4):
+        v = last_in[q].astype(F32)
+        out_ref[2 * q] = v[0:STEPS, 0:144].astype(BF16)
+        out_ref[2 * q + 1] = v[STEPS:8, 0:144].astype(BF16)
 
     x_sent = last_out.at[0]
     take_sent(x_sent, 4, x_send, own_rows, row_blocks)
@@ -624,16 +631,15 @@
     frequency = ROPE_BASE ** (-jnp.arange(128, dtype=F32) * 2.0 / HEAD_DIM)
     positions = lengths[0] + jnp.arange(STEPS, dtype=jnp.int32)
     angles = positions[:, None].astype(F32) * frequency
-    trig = jnp.tile(jnp.stack([jnp.cos(angles), jnp.sin(angles)]), (1, BEAM, 1))
 
     arrays = (
         inputs, cache_pool, lengths, block_table, parents, norm_gains,
-        w_query.T, w_key.T, w_value.T, w_out, w_gate, w_up, w_down.T, trig,
+        w_query.T, w_key.T, w_value.T, w_out, w_gate, w_up, w_down.T, jnp.cos(angles), jnp.sin(angles),
     )
     vmem = pl.BlockSpec(memory_space=pltpu.VMEM)
     specs = [pl.BlockSpec(memory_space=pltpu.HBM) for _ in arrays]
     specs[2] = pl.BlockSpec(memory_space=pltpu.SMEM)
-    specs[13] = vmem
+    specs[13:15] = [vmem, vmem]
     dma = pltpu.SemaphoreType.DMA
 
     def held(*shape, dtype=BF16):
@@ -642,7 +648,7 @@
     out = pl.pallas_call(
         functools.partial(layer_kernel, nx, ny, nx * columns),
         name="layer",
-        out_shape=jax.ShapeDtypeStruct((4, 8, 256), BF16),
+        out_shape=jax.ShapeDtypeStruct(inputs.shape, BF16),
         in_specs=specs,
         out_specs=vmem,
         scratch_shapes=[pltpu.VMEM(arrays[k].shape, arrays[k].dtype) for k in (0, 1, 3, 4, 5, 6, 7, 8, 9, 10, 11, 12)]
@@ -684,7 +690,7 @@
         + [dma(())] * 32,
         compiler_params=pltpu.CompilerParams(collective_id=0, has_side_effects=True, vmem_limit_bytes=60 << 20),
     )(*arrays)
-    return out[:, :, 0:columns].reshape(inputs.shape)
+    return out
 
 
 def solution(mesh):

time: 104 us -> 103 us (level)
  the two profiles are of different devices: /device:TPU:1 before, /device:TPU:4 now
where the time goes in v5:
time: 103 us
  Pallas kernels  100 us (97%)
  local copies, waits for them, and re-layouts  1.33 us (1%)
    pallas_call x1, Pallas kernels, body(): pl.pallas_call(functools.partial(layer_kernel, nx, ny, nx * columns), nam...  100 us

profile of v5, /device:TPU:4, one launch (start us, length us, event | category | flops | bytes accessed | tf_op | source)
XLA Modules:
  0.0 102.7 jit_solution(2316385837725399790)
XLA Ops:
  0.7 0.7 multiply_sine_fusion
  1.4 100.0 %layer.1 = bf16[8,4,144]{2,1,0:T(4,128)(2,1)} custom-call(bf16[8,4,144]{2,1,0:T(4,128)(2,1)} %inputs_ref.1, bf16[2,4,128,1024]{3,2,1,0:T(8,128)(2,1)} %cache_ref.1, s32[1]{0:T(128)} %copy.15.length_ref, s32[1,33]{1,0:T(1,128)} %table_ref.1, s32[3,8]{1,0:T(4,128)} %parents_ref.1, f32[4,144]{1,0:T(4,128)} %gains_ref.1, bf16[64,144]{1,0:T(8,128)(2,1)} %bitcast.7, ...), custom_call_target="tpu_custom_call" | custom-call | tf_op jit(solution)/shard_map/layer/pallas_call | solution.py:648
  101.4 1.3 %copy.16 = bf16[8,4,144]{2,1,0:T(4,128)(2,1)} copy(bf16[8,4,144]{2,1,0:T(4,128)(2,1)} %layer.1) | data formatting | bytes 18432
  (2 shorter events, 0.0 us)

commit v6 on v5

--- a/solution.py
+++ b/solution.py
@@ -239,27 +239,6 @@
             out.append(total)
         return out
 
-    def spread(ref, send_sem, recv_sem):
-        src = ref.at[pl.ds(first_block, row_blocks)]
-        for step in z_steps:
-            remote(src, src, send_sem, recv_sem, i, 4 * ((zj + step) % zs) + xj).start()
-
-    quarter = x_in.at[pl.ds(share * xj, share)]
-    take(quarter, x_recv)
-    for step in range(1, 4):
-        remote(quarter, quarter, x_row_send, x_row_recv, i, 4 * zj + (xj + step) % 4).start()
-    take(x_in.at[pl.ds(0, 3 * share)], x_row_recv)
-    for b in range(row_blocks):
-        rests = []
-        for p in range(nx):
-            v = x_in[p, b].astype(F32)
-            x_own[b, :, MAIN * p:MAIN * (p + 1)] = v[:, 0:MAIN]
-            rests.append(v[:, MAIN:2 * MAIN])
-        for t, v in enumerate(rest_sum(rests)):
-            x_own[b, :, MAIN * (nx + t):MAIN * (nx + t + 1)] = v
-        row_all[first_block + b] = x_own[b].astype(BF16)
-    spread(row_all, row_send, row_recv)
-
     for load in loads[5:9]:
         load.wait()
     own_b = wb_all.at[c, y]
@@ -279,6 +258,27 @@
     own_f[NARROW_AT:DOWN_AT, :] = jnp.concatenate(v, axis=1).astype(BF16)
     ring_start(1)
     to_sibling(y)
+
+    def spread(ref, send_sem, recv_sem):
+        src = ref.at[pl.ds(first_block, row_blocks)]
+        for step in z_steps:
+            remote(src, src, send_sem, recv_sem, i, 4 * ((zj + step) % zs) + xj).start()
+
+    quarter = x_in.at[pl.ds(share * xj, share)]
+    take(quarter, x_recv)
+    for step in range(1, 4):
+        remote(quarter, quarter, x_row_send, x_row_recv, i, 4 * zj + (xj + step) % 4).start()
+    take(x_in.at[pl.ds(0, 3 * share)], x_row_recv)
+    for b in range(row_blocks):
+        rests = []
+        for p in range(nx):
+            v = x_in[p, b].astype(F32)
+            x_own[b, :, MAIN * p:MAIN * (p + 1)] = v[:, 0:MAIN]
+            rests.append(v[:, MAIN:2 * MAIN])
+        for t, v in enumerate(rest_sum(rests)):
+            x_own[b, :, MAIN * (nx + t):MAIN * (nx + t + 1)] = v
+        row_all[first_block + b] = x_own[b].astype(BF16)
+    spread(row_all, row_send, row_recv)
 
     take(wa_all.at[c, pl.ds(0, ys - 1)], wa_recv)
     remote(wa_all.at[c], wa_all.at[c], wa_core_send, wa_core_recv, sibling, j).start()

time: 103 us -> 100 us (0.971)
  the two profiles are of different devices: /device:TPU:4 before, /device:TPU:1 now
where the time goes in v6:
time: 100 us
  Pallas kernels  97.3 us (97%)
  local copies, waits for them, and re-layouts  1.33 us (1%)
    pallas_call x1, Pallas kernels, body(): pl.pallas_call(functools.partial(layer_kernel, nx, ny, nx * columns), nam...  97.3 us

profile of v6, /device:TPU:1, one launch (start us, length us, event | category | flops | bytes accessed | tf_op | source)
XLA Modules:
  0.0 100.0 jit_solution(3805448365395330715)
XLA Ops:
  0.7 0.7 multiply_sine_fusion
  1.4 97.3 %layer.1 = bf16[8,4,144]{2,1,0:T(4,128)(2,1)} custom-call(bf16[8,4,144]{2,1,0:T(4,128)(2,1)} %inputs_ref.1, bf16[2,4,128,1024]{3,2,1,0:T(8,128)(2,1)} %cache_ref.1, s32[1]{0:T(128)} %copy.15.length_ref, s32[1,33]{1,0:T(1,128)} %table_ref.1, s32[3,8]{1,0:T(4,128)} %parents_ref.1, f32[4,144]{1,0:T(4,128)} %gains_ref.1, bf16[64,144]{1,0:T(8,128)(2,1)} %bitcast.7, ...), custom_call_target="tpu_custom_call" | custom-call | tf_op jit(solution)/shard_map/layer/pallas_call | solution.py:648
  98.6 1.3 %copy.16 = bf16[8,4,144]{2,1,0:T(4,128)(2,1)} copy(bf16[8,4,144]{2,1,0:T(4,128)(2,1)} %layer.1) | data formatting | bytes 18432
  (2 shorter events, 0.0 us)

commit v7 on v6

--- a/solution.py
+++ b/solution.py
@@ -148,21 +148,21 @@
     def hello(tx, ty):
         pl.semaphore_signal(barrier, inc=1, device_id=(tx, ty), device_id_type=MESH)
 
+    group = group_of(my_part)
+
+    for m in range(share):
+        p = share * xj + m
+        to = 2 * (p % ys) + p // ys
+
+        @pl.when(jnp.logical_not((to == i) & (group == j)))
+        def _():
+            hello(to, group)
+
     for step in range(1, ys):
         hello(2 * ((y + step) % ys) + c, j)
     hello(sibling, j)
     for step in range(1, zs):
         hello(i, 4 * ((zj + step) % zs) + xj)
-    group = group_of(my_part)
-
-    for m in range(share):
-        p = share * xj + m
-        to = 2 * (p % ys) + p // ys
-
-        @pl.when(jnp.logical_not((to == i) & (group == j)))
-        def _():
-            hello(to, group)
-
     for step in range(1, 4):
         hello(i, 4 * zj + (xj + step) % 4)
     waits = ys + (zs - 1) + 3 + 4 // row_blocks - jnp.where(own_rows, 1, 0)

time: 100 us -> 99.8 us (level)
  no operation moved by 1% of the time
where the time goes in v7:
time: 99.8 us; the launch traced here: 99.5 us
  Pallas kernels  96.8 us (97%)
  local copies, waits for them, and re-layouts  1.33 us (1%)
    pallas_call x1, Pallas kernels, body(): pl.pallas_call(functools.partial(layer_kernel, nx, ny, nx * columns), nam...  96.8 us

profile of v7, /device:TPU:1, one launch (start us, length us, event | category | flops | bytes accessed | tf_op | source)
XLA Modules:
  0.0 99.5 jit_solution(3886872820546491702)
XLA Ops:
  0.7 0.7 multiply_sine_fusion
  1.4 96.8 %layer.1 = bf16[8,4,144]{2,1,0:T(4,128)(2,1)} custom-call(bf16[8,4,144]{2,1,0:T(4,128)(2,1)} %inputs_ref.1, bf16[2,4,128,1024]{3,2,1,0:T(8,128)(2,1)} %cache_ref.1, s32[1]{0:T(128)} %copy.15.length_ref, s32[1,33]{1,0:T(1,128)} %table_ref.1, s32[3,8]{1,0:T(4,128)} %parents_ref.1, f32[4,144]{1,0:T(4,128)} %gains_ref.1, bf16[64,144]{1,0:T(8,128)(2,1)} %bitcast.7, ...), custom_call_target="tpu_custom_call" | custom-call | tf_op jit(solution)/shard_map/layer/pallas_call | solution.py:648
  98.2 1.3 %copy.16 = bf16[8,4,144]{2,1,0:T(4,128)(2,1)} copy(bf16[8,4,144]{2,1,0:T(4,128)(2,1)} %layer.1) | data formatting | bytes 18432
  (2 shorter events, 0.0 us)
